TPU v7x, 128 devices: a whole 4x4x4 slice. The times are simulated.
128 devices in a mesh: lon: 8 (over x_hi, y), lat: 8 (over z, core), batch: 2 (over x_lo).
Axes of the slice: x: 4 (x_hi: 2, x_lo: 2; x = x_hi * 2 + x_lo), y: 4, z: 4, core: 2. Of those that a mesh axis runs over, the one named last changes fastest.
Arguments:
- state: bfloat16 [2, 21, 256, 4096], P('batch', None, 'lat', 'lon'), may hold values from -6 to 6
- forcing: bfloat16 [2, 96, 256, 4096], P('batch', None, 'lat', 'lon'), may hold values from -6 to 6
- land_mask: int32 [256, 4096], P('lat', 'lon'), may hold values 0 or 1
- partner: int32 [4096], P('lon'), may hold values from 0 to 4095, as said below
- cotangent: bfloat16 [2, 512, 128, 2048], P('batch', None, 'lat', 'lon'), may hold values from -6 to 6
- weight_state: bfloat16 [512, 336], replicated, may hold values from -0.125 to 0.125
- weight_force: bfloat16 [512, 1536], replicated, may hold values from -0.125 to 0.125
Outputs:
- grad_state: bfloat16 [2, 21, 256, 4096], P('batch', None, 'lat', 'lon')
- grad_forcing: bfloat16 [2, 96, 256, 4096], P('batch', None, 'lat', 'lon')
- grad_wstate: float32 [512, 336], P(('lat', 'batch'))
- grad_wforce: float32 [512, 1536], P(('lat', 'batch'))
Inputs may be any that keep to these rules, and one draw needn't show every extreme that they name: partner is an involution that maps the columns of the k-th block of 512 columns onto the columns of the block k-th from the other end, in an order drawn for each pair of blocks.
All inputs are finite; a program needn't handle non-finite values. No bound on the sum of `land_mask` on one device may be relied on, other than what follows from the above.
Results may differ from a plain program's by a relative error of at most 0.0011.
Values may be sent and summed in bfloat16 or wider, within the bound.
A program may use at most 256 MiB of HBM per device.

v0:
```python
import math

import jax
import jax.numpy as jnp
from jax import lax
from jax.sharding import PartitionSpec as P


def partner_2(block, axis, distance):
    count = lax.axis_size(axis)
    route = []
    for low in range(count):
        high = low | 1 << distance
        if high != low and high < count:
            route += [(low, high), (high, low)]
    return lax.ppermute(block, axis, route)


def with_halo(cells, sides, width):
    for axis, dim in sides:
        count = lax.axis_size(axis)
        head = lax.slice_in_dim(cells, 0, width, axis=dim)
        tail = lax.slice_in_dim(cells, cells.shape[dim] - width, cells.shape[dim], axis=dim)
        cells = jnp.concatenate(
            [
                lax.ppermute(tail, axis, [(i, (i + 1) % count) for i in range(count)]),
                cells,
                lax.ppermute(head, axis, [((i + 1) % count, i) for i in range(count)]),
            ],
            axis=dim,
        )
    return cells


def on_device(state, forcing, land_mask, partner, cotangent, weight_state, weight_force):
    state_ch = state.shape[1]
    channels = state_ch + forcing.shape[1]
    cell_rows = state.shape[2]
    cell_cols = state.shape[3]
    feat_width = cotangent.shape[1]
    tok_rows = cell_rows // 2
    tok_cols = cell_cols // 2
    lon_count = lax.axis_size("lon")
    lat_count = lax.axis_size("lat")
    batch_count = lax.axis_size("batch")
    lon_at = lax.axis_index("lon")
    lat_at = lax.axis_index("lat")
    at_top = lat_at == lat_count - 1
    at_bottom = lat_at == 0
    mirror_base = (lon_count - 1 - lon_at) * cell_cols
    local_col = partner - mirror_base
    bit_count = lon_count.bit_length() - 1
    bit_order = list(range(bit_count))
    masked = jnp.concatenate([state[0], forcing[0]], axis=0) * land_mask.astype(jnp.bfloat16)
    paired = masked[:, cell_rows - 1, :]
    for bit_pos in bit_order:
        paired = partner_2(paired, "lon", bit_pos)
    fold_row = jnp.take(paired, local_col, axis=1)
    row_ext = with_halo(masked, (("lat", 1),), 1)
    south_row = jnp.where(at_bottom, jnp.zeros_like(row_ext[:, 0, :]), row_ext[:, 0, :])
    north_row = jnp.where(at_top, fold_row, row_ext[:, cell_rows + 1, :])
    row_ext = jnp.concatenate(
        [south_row[:, None, :], row_ext[:, 1 : cell_rows + 1, :], north_row[:, None, :]], axis=1
    )
    padded = with_halo(row_ext, (("lon", 2),), 1)
    planes = [[padded[:, row_par::2, col_par::2] for col_par in range(2)] for row_par in range(2)]
    windows = []
    for row_off in range(4):
        for col_off in range(4):
            plane = planes[row_off % 2][col_off % 2]
            row_start = row_off // 2
            col_start = col_off // 2
            windows.append(
                plane[:, row_start : row_start + tok_rows, col_start : col_start + tok_cols]
            )
    grad_tokens = cotangent[0]
    scale = 1.0 / math.sqrt(
        cotangent.shape[0] * batch_count * tok_rows * lat_count * tok_cols * lon_count
    )
    share = feat_width // (lat_count * batch_count)
    terms = [
        lax.dot_general(
            grad_tokens, window, (((1, 2), (1, 2)), ((), ())), preferred_element_type=jnp.float32
        )
        for window in windows
    ]
    summed = lax.psum(
        jnp.stack(terms, axis=-1).reshape(grad_tokens.shape[0], channels * 16) * scale,
        ("lon", "lat", "batch"),
    )
    kernel_own = lax.dynamic_slice_in_dim(
        summed, lax.axis_index(("lat", "batch")) * share, share, 0
    )
    grad_ext = with_halo(cotangent[0], (("lat", 1), ("lon", 2)), 1)
    south_tok = jnp.where(at_bottom, jnp.zeros_like(grad_ext[:, :1, :]), grad_ext[:, :1, :])
    north_tok = jnp.where(at_top, jnp.zeros_like(grad_ext[:, -1:, :]), grad_ext[:, -1:, :])
    grad_ext = jnp.concatenate([south_tok, grad_ext[:, 1 : tok_rows + 1, :], north_tok], axis=1)
    weights = jnp.concatenate([weight_state, weight_force], axis=1)
    spread_all = lax.dot_general(
        weights, grad_ext, (((0,), (0,)), ((), ())), preferred_element_type=jnp.float32
    )
    spread_all = spread_all.reshape(channels, 4, 4, tok_rows + 2, tok_cols + 2)
    parity_terms = (((1, 1), (3, 0)), ((0, 2), (2, 1)))
    fold_cols = []
    for col_par in range(2):
        acc_fold = jnp.zeros((channels, tok_cols), jnp.float32)
        for col_off, col_start in parity_terms[col_par]:
            acc_fold = (
                acc_fold + spread_all[:, 3, col_off, tok_rows, col_start : col_start + tok_cols]
            )
        fold_cols.append(acc_fold)
    fold_part = jnp.stack(fold_cols, axis=-1).reshape(channels, cell_cols)
    arrived = jnp.zeros((channels, cell_cols), jnp.float32).at[:, local_col].set(fold_part)
    for bit_pos in bit_order:
        arrived = partner_2(arrived.astype(jnp.bfloat16), "lon", bit_pos).astype(arrived.dtype)
    arrived = jnp.where(at_top, arrived, jnp.zeros_like(arrived))
    mask_float = land_mask.astype(jnp.float32)
    row_blocks = []
    for row_par in range(2):
        col_blocks = []
        for col_par in range(2):
            acc_cells = jnp.zeros((channels, tok_rows, tok_cols), jnp.float32)
            for row_off, row_start in parity_terms[row_par]:
                for col_off, col_start in parity_terms[col_par]:
                    acc_cells = (
                        acc_cells
                        + spread_all[
                            :,
                            row_off,
                            col_off,
                            row_start : row_start + tok_rows,
                            col_start : col_start + tok_cols,
                        ]
                    )
            if row_par == 1:
                acc_cells = acc_cells.at[:, tok_rows - 1, :].add(arrived[:, col_par::2])
            mask_plane = mask_float[row_par::2, col_par::2]
            col_blocks.append((acc_cells * mask_plane).astype(jnp.bfloat16))
        row_blocks.append(jnp.stack(col_blocks, axis=-1))
    result = jnp.stack(row_blocks, axis=2).reshape(channels, cell_rows, cell_cols)
    return (
        result[None, :state_ch],
        result[None, state_ch:],
        kernel_own[:, : state_ch * 16],
        kernel_own[:, state_ch * 16 :],
    )


def solution(mesh):
    in_specs = (
        P("batch", None, "lat", "lon"),
        P("batch", None, "lat", "lon"),
        P("lat", "lon"),
        P("lon"),
        P("batch", None, "lat", "lon"),
        P(),
        P(),
    )
    out_specs = (
        P("batch", None, "lat", "lon"),
        P("batch", None, "lat", "lon"),
        P(("lat", "batch"), None),
        P(("lat", "batch"), None),
    )
    return jax.shard_map(
        on_device, mesh=mesh, in_specs=in_specs, out_specs=out_specs, check_vma=False
    )
```

profile of v0, /device:TPU:0, one launch (start us, length us, event | category | flops | bytes accessed | tf_op | source)
XLA Modules:
  0.0 741.4 jit_solution(12922439610931023367)
XLA Ops:
  7.2 7.8 %copy.200 = bf16[1,512,16,256]{1,3,2,0:T(8,128)(2,1)} copy(bf16[1,512,16,256]{3,2,1,0:T(8,128)(2,1)} %param.15) | data formatting | bytes 8388608 | tf_op args[4]
  37.2 7.6 %copy.251 = bf16[512,16,256]{0,2,1:T(8,128)(2,1)} copy(bf16[512,16,256]{2,1,0:T(8,128)(2,1)} %bitcast.187) | data formatting | bytes 8388608 | tf_op jit(solution)/shard_map/squeeze | solution.py:94
  59.3 6.6 pad_maximum_fusion.1
  68.1 22.9 %fusion = f32[1872,18,258]{2,0,1:T(8,128)} fusion(bf16[512,1,258]{0,2,1:T(8,128)(2,1)} %get-tuple-element.65, bf16[512,16,258]{0,2,1:T(8,128)(2,1)S(1)} %slice.297, bf16[512,1,258]{0,2,1:T(8,128)(2,1)S(1)} %get-tuple-element.64, bf16[512,1536]{0,1:T(8,128)(2,1)} %copy.199, bf16[512,336]{0,1:T(8,128)(2,1)} %param.16), kind=kOutput, calls=%fused_computation.4 | convolution fusion | flops 8920313856 | bytes 41446656 | tf_op jit(solution)/shard_map/dot_general | solution.py:99
  91.0 58.6 %reshape.251 = f32[117,4,4,18,258]{4,2,1,0,3:T(4,128)} reshape(f32[1872,18,258]{2,0,1:T(8,128)} %fusion) | data formatting | bytes 69548544 | tf_op jit(solution)/shard_map/reshape | solution.py:102
  149.7 72.5 %fusion.36 = (f32[117,1,1,16,256]{4,2,1,0,3:T(1,128)}, f32[117,1,1,16,256]{4,2,1,0,3:T(1,128)}, f32[117,1,1,16,256]{4,2,1,0,3:T(1,128)}, f32[117,1,1,16,256]{4,2...) fusion(f32[117,4,4,18,258]{4,2,1,0,3:T(4,128)} %reshape.251), kind=kLoop, calls=%fused_computation.92 | loop fusion | bytes 61341696 | tf_op jit(solution)/shard_map/slice | solution.py:127
  232.7 6.1 copy.305
  238.7 6.1 copy.303
  244.8 6.1 copy.304
  251.0 6.1 copy.302
  257.1 6.1 copy.301
  263.2 6.1 copy.299
  269.2 6.1 copy.300
  275.3 7.4 fusion.6
  287.3 6.1 copy.309
  293.4 6.1 copy.307
  299.5 6.1 copy.308
  321.0 6.2 copy.314
  330.8 6.2 copy.311
  341.8 7.6 %pad_maximum_fusion = bf16[117,34,514]{2,0,1:T(8,128)(2,1)} fusion(bf16[117,34,1]{2,0,1:T(8,128)(2,1)S(1)} %copy.229, bf16[117,1,512]{2,0,1:T(8,128)(2,1)S(1)} %fusion.32, bf16[117,32,512]{2,0,1:T(8,128)(2,1)} %copy-done.3, bf16[117,1,512]{2,0,1:T(8,128)(2,1)S(1)} %broadcast_select_fusion, bf16[117,34,1]{2,0,1:T(8,128)(2,1)S(1)} %copy.228), kind=kLoop, calls=%fused_computation.2 | loop fusion | flops 20446920 | bytes 8178768 | tf_op jit(solution)/shard_map/concatenate | solution.py:24
  349.4 42.5 %slice.271 = bf16[117,17,257]{2,0,1:T(8,128)(2,1)S(1)} slice(bf16[117,34,514]{2,0,1:T(8,128)(2,1)} %pad_maximum_fusion), slice={[0:117:1], [0:34:2], [0:514:2]} | slice | bytes 2044692 | tf_op jit(solution)/shard_map/slice | solution.py:66
  392.0 42.9 %slice.273 = bf16[117,17,257]{2,0,1:T(8,128)(2,1)S(1)} slice(bf16[117,34,514]{2,0,1:T(8,128)(2,1)} %pad_maximum_fusion), slice={[0:117:1], [0:34:2], [1:514:2]} | slice | bytes 2044692 | tf_op jit(solution)/shard_map/slice | solution.py:66
  442.4 41.6 %slice.277 = bf16[117,17,257]{2,0,1:T(8,128)(2,1)} slice(bf16[117,34,514]{2,0,1:T(8,128)(2,1)} %pad_maximum_fusion), slice={[0:117:1], [1:34:2], [0:514:2]} | slice | bytes 2044692 | tf_op jit(solution)/shard_map/slice | solution.py:66
  484.0 43.0 %slice.279 = bf16[117,17,257]{2,0,1:T(8,128)(2,1)S(1)} slice(bf16[117,34,514]{2,0,1:T(8,128)(2,1)} %pad_maximum_fusion), slice={[0:117:1], [1:34:2], [1:514:2]} | slice | bytes 2044692 | tf_op jit(solution)/shard_map/slice | solution.py:66
  546.1 28.3 %stack.103 = f32[512,117,16]{0,2,1:T(8,128)} concatenate(f32[512,117,1]{0,2,1:T(1,128)S(1)} %stack.87, f32[512,117,1]{0,2,1:T(1,128)S(1)} %stack.88, f32[512,117,1]{0,2,1:T(1,128)S(1)} %stack.89, f32[512,117,1]{0,2,1:T(1,128)S(1)} %stack.90, f32[512,117,1]{0,2,1:T(1,128)S(1)} %stack.91, f32[512,117,1]{0,2,1:T(1,128)S(1)} %stack.92, f32[512,117,1]{0,2,1:T(1,128)S(1)} %stack.93, ...), dimensions={2} | concatenate | bytes 7667712 | tf_op jit(solution)/shard_map/stack | solution.py:88
  587.9 5.7 collective-permute-done.6
  604.3 8.6 %copy.220 = bf16[21,16,2,256,2]{0,4,3,2,1:T(2,128)(2,1)} copy(bf16[21,16,2,256,2]{0,3,1,4,2:T(8,128)(2,1)} %slice_maximum_fusion) | data formatting | bytes 1376256 | tf_op jit(solution)/shard_map/slice | solution.py:142
  612.9 4.9 copy.246
  617.8 5.0 pad_maximum_fusion.2
  622.8 8.6 %copy.221 = bf16[96,16,2,256,2]{0,4,3,2,1:T(2,128)(2,1)} copy(bf16[96,16,2,256,2]{0,3,1,4,2:T(8,128)(2,1)} %pad_maximum_fusion.2) | data formatting | bytes 6291456 | tf_op jit(solution)/shard_map/slice | solution.py:143
  631.4 7.4 copy.247
  638.7 91.6 %all-reduce.2.cloned.1.call-done = f32[512,1872]{0,1:T(8,128)} async-done(((f32[512,1872]{0,1:T(8,128)}), f32[512,1872]{0,1:T(8,128)}) %all-reduce.2.cloned.1.call-update) | async-done | bytes 3833872 | tf_op jit(solution)/shard_map/psum | solution.py:87
  (158 shorter events, 132.0 us)
Async XLA Ops:
  7.2 13.2 %copy-start.21 = (s32[32,512]{1,0:T(8,128)S(1)}, s32[32,512]{1,0:T(8,128)}, u32[]{:S(2)}) copy-start(s32[32,512]{1,0:T(8,128)} %param.13) | copy-start | bytes 196612
  7.2 723.1 %all-reduce.2.cloned.1.call-start = ((), (), s32[]{:S(2)}) async-start(), calls=%async_computation | async-start | bytes 7667712 | tf_op jit(solution)/shard_map/psum | solution.py:87
  7.2 13.2 %copy-start.13 = (bf16[1,96,32,512]{3,2,1,0:T(8,128)(2,1)S(1)}, bf16[1,96,32,512]{3,2,1,0:T(8,128)(2,1)}, u32[]{:S(2)}) copy-start(bf16[1,96,32,512]{3,2,1,0:T(8,128)(2,1)} %param.12) | copy-start | bytes 9437188
  16.8 30.8 %collective-permute-start.1 = (bf16[512,1,256]{0,2,1:T(8,128)(2,1)}, bf16[512,1,256]{0,2,1:T(8,128)(2,1)S(1)}, u32[]{:S(2)}, u32[]{:S(2)}) collective-permute-start(bf16[512,1,256]{0,2,1:T(8,128)(2,1)} %get-tuple-element.69), channel_id=1, source_target_pairs={{2,0},{4,2},{6,4},{8,6},{10,8},{12,10},{14,12},{0,14},{3,1},{5,3},... | collective-permute-start | bytes 786440 | tf_op jit(solution)/shard_map/ppermute | solution.py:28
  20.4 27.3 %collective-permute-start = (bf16[512,1,256]{0,2,1:T(8,128)(2,1)}, bf16[512,1,256]{0,2,1:T(8,128)(2,1)}, u32[]{:S(2)}, u32[]{:S(2)}) collective-permute-start(bf16[512,1,256]{0,2,1:T(8,128)(2,1)} %get-tuple-element.68), channel_id=1, source_target_pairs={{0,2},{2,4},{4,6},{6,8},{8,10},{10,12},{12,14},{14,0},{1,3},{3,5},... | collective-permute-start | bytes 786440 | tf_op jit(solution)/shard_map/ppermute | solution.py:26
  20.4 1.8 copy-start.18
  22.6 9.3 %copy-start.22 = (s32[512]{0:T(512)S(1)}, s32[512]{0:T(512)}, u32[]{:S(2)}) copy-start(s32[512]{0:T(512)} %param.14) | copy-start | bytes 6148
  22.6 13.0 %copy-start.14 = (bf16[512,1536]{1,0:T(8,128)(2,1)S(1)}, bf16[512,1536]{1,0:T(8,128)(2,1)}, u32[]{:S(2)}) copy-start(bf16[512,1536]{1,0:T(8,128)(2,1)} %param.17) | copy-start | bytes 4718596
  24.8 1.9 copy-start.3
  27.4 280.7 %collective-permute-start.11 = (bf16[117,1,512]{2,0,1:T(8,128)(2,1)}, bf16[117,1,512]{2,0,1:T(8,128)(2,1)}, u32[]{:S(2)}, u32[]{:S(2)}) collective-permute-start(bf16[117,1,512]{2,0,1:T(8,128)(2,1)} %get-tuple-element.74), channel_id=1, source_target_pairs={{2,0},{4,2},{6,4},{8,6},{10,8},{12,10},{14,12},{0,14},{3,1},{5,3},... | collective-permute-start | bytes 359432 | tf_op jit(solution)/shard_map/ppermute | solution.py:28
  30.3 14.4 %collective-permute-start.8 = (bf16[117,512]{1,0:T(8,128)(2,1)S(1)}, bf16[117,512]{1,0:T(8,128)(2,1)S(1)}, u32[]{:S(2)}, u32[]{:S(2)}) collective-permute-start(bf16[117,512]{1,0:T(8,128)(2,1)S(1)} %get-tuple-element.73), channel_id=1, source_target_pairs={{0,16},{16,0},{32,48},{48,32},{64,80},{80,64},{96,112},{112,96},{1... | collective-permute-start | bytes 359432 | tf_op jit(solution)/shard_map/ppermute | solution.py:16
  31.9 19.9 %collective-permute-start.7 = (bf16[117,1,512]{2,0,1:T(8,128)(2,1)S(1)}, bf16[117,1,512]{2,0,1:T(8,128)(2,1)S(1)}, u32[]{:S(2)}, u32[]{:S(2)}) collective-permute-start(bf16[117,1,512]{2,0,1:T(8,128)(2,1)S(1)} %get-tuple-element.72), channel_id=1, source_target_pairs={{0,2},{2,4},{4,6},{6,8},{8,10},{10,12},{12,14},{14,0},{1,3},{3,5},... | collective-permute-start | bytes 359432 | tf_op jit(solution)/shard_map/ppermute | solution.py:26
  44.8 14.6 %copy-start.2 = (bf16[1,512,16,256]{1,3,2,0:T(8,128)(2,1)S(1)}, bf16[1,512,16,256]{1,3,2,0:T(8,128)(2,1)}, u32[]{:S(2)}) copy-start(bf16[1,512,16,256]{1,3,2,0:T(8,128)(2,1)} %copy.200) | copy-start | bytes 12582916
  44.8 7.0 collective-permute-start.9
  48.7 5.8 collective-permute-start.3
  51.8 7.6 %collective-permute-start.2 = (bf16[512,18,1]{0,2,1:T(2,128)(2,1)S(1)}, bf16[512,18,1]{0,2,1:T(2,128)(2,1)S(1)}, u32[]{:S(2)}, u32[]{:S(2)}) collective-permute-start(bf16[512,18,1]{0,2,1:T(2,128)(2,1)S(1)} %get-tuple-element.66), channel_id=1, source_target_pairs={{0,16},{16,32},{32,48},{48,64},{64,80},{80,96},{96,112},{112,0},{1... | collective-permute-start | bytes 55304 | tf_op jit(solution)/shard_map/ppermute | solution.py:26
  51.8 253.8 %collective-permute-start.10 = (bf16[117,512]{1,0:T(8,128)(2,1)}, bf16[117,512]{1,0:T(8,128)(2,1)}, u32[]{:S(2)}, u32[]{:S(2)}) collective-permute-start(bf16[117,512]{1,0:T(8,128)(2,1)} %collective-permute-done.9), channel_id=1, source_target_pairs={{0,64},{64,0},{16,80},{80,16},{32,96},{96,32},{48,112},{112,48},{1... | collective-permute-start | bytes 359432 | tf_op jit(solution)/shard_map/ppermute | solution.py:16
  228.0 351.3 %collective-permute-start.4 = (bf16[117,512]{0,1:T(8,128)(2,1)}, bf16[117,512]{0,1:T(8,128)(2,1)}, u32[]{:S(2)}, u32[]{:S(2)}) collective-permute-start(bf16[117,512]{0,1:T(8,128)(2,1)} %convert_element_type.45), channel_id=1, source_target_pairs={{0,16},{16,0},{32,48},{48,32},{64,80},{80,64},{96,112},{112,96},{1... | collective-permute-start | bytes 359432 | tf_op jit(solution)/shard_map/ppermute | solution.py:16
  313.6 27.0 %collective-permute-start.13 = (bf16[117,34,1]{0,1,2:T(8,128)(2,1)S(1)}, bf16[117,34,1]{0,1,2:T(8,128)(2,1)S(1)}, u32[]{:S(2)}, u32[]{:S(2)}) collective-permute-start(bf16[117,34,1]{0,1,2:T(8,128)(2,1)S(1)} %copy.227), channel_id=1, source_target_pairs={{16,0},{32,16},{48,32},{64,48},{80,64},{96,80},{112,96},{0,112},{1... | collective-permute-start | bytes 23876 | tf_op jit(solution)/shard_map/ppermute | solution.py:28
  314.2 27.0 %collective-permute-start.12 = (bf16[117,34,1]{0,1,2:T(8,128)(2,1)S(1)}, bf16[117,34,1]{0,1,2:T(8,128)(2,1)S(1)}, u32[]{:S(2)}, u32[]{:S(2)}) collective-permute-start(bf16[117,34,1]{0,1,2:T(8,128)(2,1)S(1)} %copy.226), channel_id=1, source_target_pairs={{0,16},{16,32},{32,48},{48,64},{64,80},{80,96},{96,112},{112,0},{1... | collective-permute-start | bytes 23876 | tf_op jit(solution)/shard_map/ppermute | solution.py:26
  321.0 6.2 copy-start.10
  330.8 6.2 copy-start.9
  392.0 46.7 %copy-start.4 = (bf16[117,17,257]{2,0,1:T(8,128)(2,1)}, bf16[117,17,257]{2,0,1:T(8,128)(2,1)S(1)}, u32[]{:S(2)}) copy-start(bf16[117,17,257]{2,0,1:T(8,128)(2,1)S(1)} %slice.271) | copy-start | bytes 3067042
  434.9 3.8 copy-start
  527.0 3.7 copy-start.1
  579.2 2.6 copy-start.8
  579.3 8.2 %copy-start.11 = (bf16[117,16,256,1]{0,2,1,3:T(8,128)(2,1)S(1)}, bf16[117,16,256,1]{0,2,1,3:T(8,128)(2,1)}, u32[]{:S(2)}) copy-start(bf16[117,16,256,1]{0,2,1,3:T(8,128)(2,1)} %get-tuple-element.79) | copy-start | bytes 2875396
  579.3 8.2 %copy-start.12 = (bf16[117,16,256,1]{0,2,1,3:T(8,128)(2,1)S(1)}, bf16[117,16,256,1]{0,2,1,3:T(8,128)(2,1)}, u32[]{:S(2)}) copy-start(bf16[117,16,256,1]{0,2,1,3:T(8,128)(2,1)} %get-tuple-element.80) | copy-start | bytes 2875396
  579.3 7.4 %collective-permute-start.5 = (bf16[117,512]{0,1:T(8,128)(2,1)}, bf16[117,512]{0,1:T(8,128)(2,1)S(1)}, u32[]{:S(2)}, u32[]{:S(2)}) collective-permute-start(bf16[117,512]{0,1:T(8,128)(2,1)} %collective-permute-done.4), channel_id=1, source_target_pairs={{0,32},{32,0},{16,48},{48,16},{64,96},{96,64},{80,112},{112,80},{1... | collective-permute-start | bytes 359432 | tf_op jit(solution)/shard_map/ppermute | solution.py:16
  586.7 6.9 collective-permute-start.6
  587.4 9.6 %copy-start.19 = (f32[16,256]{1,0:T(8,128)S(1)}, f32[16,256]{1,0:T(8,128)}, u32[]{:S(2)}) copy-start(f32[16,256]{1,0:T(8,128)} %slice.257) | copy-start | bytes 49156
  587.4 9.6 %copy-start.20 = (f32[16,256]{1,0:T(8,128)S(1)}, f32[16,256]{1,0:T(8,128)}, u32[]{:S(2)}) copy-start(f32[16,256]{1,0:T(8,128)} %slice.264) | copy-start | bytes 49156
  (6 other events, 7.7 us)
Sparse Core Ops, SparseCore 0:
  579.4 150.8 all-reduce.1
where the time goes:
time: 754 us; the launch traced here: 741 us
  local copies, waits for them, and re-layouts  495 us (66%)
  waiting for transfers between devices  102 us (14%)
  other arithmetic  63.3 us (8%)
  matrix products  43.5 us (6%)
  starting transfers between devices  22.2 us (3%)
  between operations  14.9 us (2%)
    slice x4, local copies, waits for them, and re-layouts, on_device(): padded[:, row_par::2, col_par::2]  170 us
    unnamed x70, local copies, waits for them, and re-layouts  120 us
    psum x1, waiting for transfers between devices, on_device(): lax.psum(jnp.stack(terms, axis=-1).reshape(grad_tokens.shape[0], channels...  91.6 us
    slice x1, local copies, waits for them, and re-layouts, on_device(): spread_all[:, row_off, col_off, row_start:row_start + tok_rows, col_start...  72.5 us
    reshape x1, local copies, waits for them, and re-layouts, on_device(): spread_all = spread_all.reshape(channels, 4, 4, tok_rows + 2, tok_cols + 2)  58.6 us
    another operation x17, local copies, waits for them, and re-layouts, on_device(): jnp.stack(terms, axis=-1).reshape(grad_tokens.shape[0], channels * 16)  32.4 us
    dot_general x1, matrix products, on_device(): lax.dot_general(weights, grad_ext, (((0,), (0,)), ((), ())), preferred_el...  22.9 us
    dot_general x16, matrix products, on_device(): lax.dot_general(grad_tokens, window, (((1, 2), (1, 2)), ((), ())), prefer...  20.6 us
  transfers between devices with their start and end apart: 15, of which 3 were waited for; matrix products, arithmetic and copies ran while one was open for 79% of the time, Pallas kernels for 0%

commit v1 on v0

v1 whole, which is shorter than its diff:
```python
import functools
import math

import jax
import jax.numpy as jnp
from jax import lax
from jax.experimental import pallas as pl
from jax.experimental.pallas import tpu as pltpu
from jax.sharding import PartitionSpec as P

SC = 21
CP = 128
F0 = 24
F32 = jnp.float32
BF16 = jnp.bfloat16
JORD = (1, 2, 0, 3)
ROWS = ((1, 0, 0), (2, 1, 1), (0, 1, 0), (3, 0, 1))


def iota(shape, dim):
    return lax.broadcasted_iota(jnp.int32, shape, dim)


def dot(a, b):
    return lax.dot_general(a, b, (((1,), (0,)), ((), ())), preferred_element_type=F32)


def dot_nt(a, b):
    return lax.dot_general(a, b, (((1,), (1,)), ((), ())), preferred_element_type=F32)


def put(buf, at, value):
    for t in range(value.shape[1] // 128):
        buf[t, at, :] = value[:, t * 128:(t + 1) * 128]


def get(buf, at):
    return jnp.concatenate([buf[t, at, :] for t in range(buf.shape[0])], axis=1)


def main_kernel(
    state, force, mask, local_col, cot, wst, wf,
    g_out, xs_out, xf_out,
    raw, sbuf, planes, craw, cf32, cot_a, cot_b, wcat, gbuf, wstage, wspad, perm, permt, fold_sel,
    rxs, rxn, rmir, rcs, rcn, sx, rxw, rxe, sc, rcw, rce, sfold, rfold,
    in_sem, out_sem, send, recv,
):
    lon_n = lax.axis_size("lon")
    lat_n = lax.axis_size("lat")
    lon = lax.axis_index("lon")
    lat = lax.axis_index("lat")
    at_top = lat == lat_n - 1
    at_bottom = lat == 0
    north = {"lat": lax.rem(lat + 1, lat_n)}
    south = {"lat": lax.rem(lat + lat_n - 1, lat_n)}
    east = {"lon": lax.rem(lon + 1, lon_n)}
    west = {"lon": lax.rem(lon + lon_n - 1, lon_n)}
    mirror = {"lon": lon_n - 1 - lon}

    cuts = [(state, 0, 0, SC * 32)]
    for k in range(6):
        cuts.append((force, k * 512, F0 * 32 + k * 512, 512))
    loads = []
    for n, (src, at, to, rows) in enumerate(cuts):
        loads.append(pltpu.make_async_copy(src.at[pl.ds(at, rows)], raw.at[pl.ds(to, rows)], in_sem.at[n]))
    loads.append(pltpu.make_async_copy(cot, craw, in_sem.at[7]))
    loads.append(pltpu.make_async_copy(wst, wspad.at[pl.ds(0, 336)], in_sem.at[8]))
    loads.append(pltpu.make_async_copy(wf, wstage, in_sem.at[9]))
    for copy in loads:
        copy.start()

    barrier = pltpu.get_barrier_semaphore()
    for peer in (north, south, east, west, mirror):
        pl.semaphore_signal(barrier, inc=1, device_id=peer, device_id_type=pl.DeviceIdType.MESH)
    pl.semaphore_wait(barrier, 5)

    def remote(n, src, dst, peer):
        return pltpu.make_async_remote_copy(
            src_ref=src, dst_ref=dst, send_sem=send.at[n], recv_sem=recv.at[n],
            device_id=peer, device_id_type=pl.DeviceIdType.MESH,
        )

    row5, col5 = iota((512, 512), 0), iota((512, 512), 1)
    deint = jnp.where(lax.rem(row5, 2) * 256 + lax.div(row5, 2) == col5, 1.0, 0.0).astype(BF16)
    perm[...] = deint
    permt[...] = jnp.where(lax.rem(col5, 2) * 256 + lax.div(col5, 2) == row5, 1.0, 0.0).astype(BF16)

    put(sbuf, pl.ds(SC * 32, 3 * 32), jnp.zeros((96, 512), F32))
    put(sbuf, pl.ds(120 * 32, 8 * 32), jnp.zeros((256, 512), F32))
    mask_bf = mask[...].astype(F32).astype(BF16)
    for n, (_, _, to, rows) in enumerate(cuts):
        loads[n].wait()
        x = raw[pl.ds(to, rows), :].reshape(rows // 32, 32, 512) * mask_bf[None]
        put(sbuf, pl.ds(to, rows), dot(x.reshape(rows, 512), perm[...]))

    lane128 = iota((CP, 128), 1)
    lane256 = iota((CP, 256), 1)

    def four(even, odd):
        left = jnp.where(lane256 == 0, 0.0, pltpu.roll(odd, 1, 1))
        right = jnp.where(lane256 == 255, 0.0, pltpu.roll(even, 255, 1))
        return even, odd, left, right

    def put_row(parity, slot, even, odd):
        at = pl.multiple_of(slot * 256, 256)
        for j, part in enumerate(four(even, odd)):
            planes[pl.ds((parity * 4 + j) * CP, CP), pl.ds(at, 256)] = part.astype(BF16)

    def edge_of(acc, r, even, odd):
        acc = jnp.where(lane128 == r + 1, even[:, 0:1], acc)
        return jnp.where(lane128 == 65 + r, odd[:, 255:256], acc)

    def split_rows(a, acc):
        for parity in range(2):
            r = 2 * a + parity
            x = get(sbuf, pl.ds(r, CP, stride=32))
            even, odd = x[:, :256], x[:, 256:]
            put_row(parity, a + parity, even, odd)
            acc = edge_of(acc, r, even, odd)
        return acc

    edges = lax.fori_loop(0, 16, split_rows, jnp.zeros((CP, 128), F32))

    x_north = remote(0, planes.at[pl.ds(512, 512), pl.ds(16 * 256, 256)], rxs, north)
    x_south = remote(1, planes.at[pl.ds(0, 512), pl.ds(0, 256)], rxn, south)
    x_mirror = remote(2, planes.at[pl.ds(512, 256), pl.ds(16 * 256, 256)], rmir, mirror)
    x_north.start()
    x_south.start()

    @pl.when(at_top)
    def _():
        x_mirror.start()

    loads[7].wait()

    def widen(k, _):
        at = pl.multiple_of(k * 512, 512)
        put(cf32, pl.ds(at, 512), craw[pl.ds(at, 512), :].astype(F32))
        return 0

    lax.fori_loop(0, 16, widen, 0)
    clane = iota((512, 128), 1)

    def split_tokens(a, acc):
        x = get(cf32, pl.ds(a, 512, stride=16))
        xb = x.astype(BF16)
        cot_a[:, pl.ds(pl.multiple_of(a * 256, 256), 256)] = xb
        cot_b[pl.ds(pl.multiple_of((a + 1) * 512, 512), 512), :] = xb
        acc = jnp.where(clane == a + 1, x[:, 0:1], acc)
        return jnp.where(clane == 65 + a, x[:, 255:256], acc)

    cedges = lax.fori_loop(0, 16, split_tokens, jnp.zeros((512, 128), F32))
    sc[...] = cedges.astype(BF16)
    c_north = remote(3, cot_b.at[pl.ds(16 * 512, 512)], rcs, north)
    c_south = remote(4, cot_b.at[pl.ds(512, 512)], rcn, south)
    c_north.start()
    c_south.start()

    def tile(n, pair):
        _, parity, off = ROWS[n]
        rows = planes[pl.ds((parity * 4 + pair * 2) * CP, 2 * CP), pl.ds(off * 256, 4096)]
        return dot_nt(cot_a[...], rows)

    gbuf[0] = tile(0, 0)
    gbuf[1] = tile(1, 0)

    natural = jnp.where(row5 == local_col[...], 1.0, 0.0).astype(BF16)
    half = dot(natural, perm[...]).astype(BF16)
    fold_sel[...] = dot(permt[...], half).astype(BF16)

    x_north.wait()
    x_south.wait()
    zero16 = jnp.zeros((), BF16)
    planes[pl.ds(512, 512), pl.ds(0, 256)] = jnp.where(at_bottom, zero16, rxs[...])
    planes[pl.ds(0, 512), pl.ds(16 * 256, 256)] = rxn[...]

    @pl.when(at_top)
    def _():
        x_mirror.wait()
        top = jnp.concatenate([rmir[pl.ds(0, CP), :], rmir[pl.ds(CP, CP), :]], axis=1)
        folded = dot(top, fold_sel[...])
        put_row(0, 16, folded[:, :256], folded[:, 256:])

    acc = edges
    low_e = planes[pl.ds(512, CP), pl.ds(0, 128)].astype(F32)
    low_o = planes[pl.ds(512 + CP, CP), pl.ds(128, 128)].astype(F32)
    high_e = planes[pl.ds(0, CP), pl.ds(16 * 256, 128)].astype(F32)
    high_o = planes[pl.ds(CP, CP), pl.ds(16 * 256 + 128, 128)].astype(F32)
    acc = jnp.where(lane128 == 0, low_e[:, 0:1], acc)
    acc = jnp.where(lane128 == 64, low_o[:, 127:128], acc)
    acc = jnp.where(lane128 == 33, high_e[:, 0:1], acc)
    acc = jnp.where(lane128 == 97, high_o[:, 127:128], acc)
    sx[...] = acc.astype(BF16)
    x_east = remote(5, sx, rxw, east)
    x_west = remote(6, sx, rxe, west)
    x_east.start()
    x_west.start()

    c_north.wait()
    c_south.wait()
    cot_b[pl.ds(0, 512), :] = jnp.where(at_bottom, zero16, rcs[...])
    cot_b[pl.ds(17 * 512, 512), :] = jnp.where(at_top, zero16, rcn[...])
    low = cot_b[pl.ds(0, 512), :].astype(F32)
    high = cot_b[pl.ds(17 * 512, 512), :].astype(F32)
    acc = sc[...].astype(F32)
    acc = jnp.where(clane == 0, low[:, 0:1], acc)
    acc = jnp.where(clane == 64, low[:, 255:256], acc)
    acc = jnp.where(clane == 17, high[:, 0:1], acc)
    acc = jnp.where(clane == 81, high[:, 255:256], acc)
    sc[...] = acc.astype(BF16)
    c_east = remote(7, sc, rcw, east)
    c_west = remote(8, sc, rce, west)
    c_east.start()
    c_west.start()

    gbuf[2] = tile(2, 0)
    gbuf[3] = tile(3, 0)
    x_east.wait()
    x_west.wait()
    side = jnp.concatenate(
        [jnp.where(lane128 >= 64, rxw[...], zero16), jnp.where(lane128 < 64, rxe[...], zero16)], axis=0
    )
    lrow, lcol = iota((128, 128), 0), iota((128, 128), 1)
    for n in range(4):
        i = ROWS[n][0]
        first = (lrow >= 1) & (lrow <= 16) & (lcol == 62 + 2 * lrow + i)
        last = (lrow >= 65) & (lrow <= 80) & (lcol == 2 * lrow - 130 + i)
        spread = jnp.where(first | last, 1.0, 0.0).astype(BF16)
        moved = dot(sc[...], spread).astype(BF16)
        gbuf[4 + n] = tile(n, 1) + dot_nt(moved, side)
    g_copy = pltpu.make_async_copy(gbuf, g_out, out_sem.at[8])
    g_copy.start()

    loads[8].wait()
    loads[9].wait()
    wspad[pl.ds(336, 48), :] = jnp.zeros((48, 512), BF16)
    pick = jnp.where(lax.rem(lrow, 8) * 16 + lax.div(lrow, 8) == lcol, 1.0, 0.0).astype(BF16)
    for o in range(16):
        put(sbuf, pl.ds(o * CP + 120, 8), jnp.zeros((8, 512), F32))
    for kb in range(15):
        if kb < 3:
            got = dot(pick, wspad[pl.ds(kb * 128, 128), :])
        else:
            got = dot_nt(pick, wstage[:, pl.ds((kb - 3) * 128, 128)])
        for o in range(16):
            put(sbuf, pl.ds(o * CP + kb * 8, 8), got[o * 8:o * 8 + 8, :])
    for parity in range(2):
        for j in range(4):
            for k, i in enumerate(((3, 1), (2, 0))[parity]):
                wcat[pl.ds((parity * 4 + j) * CP, CP), pl.ds(k * 512, 512)] = get(
                    sbuf, pl.ds((i * 4 + JORD[j]) * CP, CP)
                ).astype(BF16)

    c_east.wait()
    c_west.wait()
    z_west, z_east = [], []
    for parity in range(2):
        for j, src, out in ((3, rcw, z_west), (2, rce, z_east)):
            w_rows = wcat[pl.ds((parity * 4 + j) * CP, CP), :]
            first = dot(w_rows[:, :512], src[...])
            second = dot(w_rows[:, 512:], src[...])
            out.append(first + pltpu.roll(second, 127, 1))

    def token_row(s, parity):
        tokens = cot_b[pl.ds(pl.multiple_of(s * 512, 512), 1024), :]
        u = dot(wcat[pl.ds(parity * 512, 512), :], tokens)
        u1, u2, u0, u3 = (u[k * CP:(k + 1) * CP] for k in range(4))
        zw = pltpu.roll(z_west[parity], 64 - s, 1)
        ze = pltpu.roll(z_east[parity], 127 - s, 1)
        r3 = pltpu.roll(u3, 1, 1)
        r0 = pltpu.roll(u0, 255, 1)
        r3 = jnp.concatenate([jnp.where(lane128 == 0, zw, r3[:, :128]), r3[:, 128:]], axis=1)
        r0 = jnp.concatenate([r0[:, :128], jnp.where(lane128 == 127, ze, r0[:, 128:])], axis=1)
        return jnp.concatenate([u1 + r3, u2 + r0], axis=1)

    sfold[...] = token_row(16, 0).astype(BF16)
    g_mirror = remote(9, sfold, rfold, mirror)

    @pl.when(at_top)
    def _():
        g_mirror.start()

    put(sbuf, pl.ds(31, CP, stride=32), token_row(16, 1))
    put(sbuf, pl.ds(0, CP, stride=32), token_row(0, 0))

    def rows_of(s, _):
        put(sbuf, pl.ds(2 * s, CP, stride=32), token_row(s, 0))
        put(sbuf, pl.ds(2 * s - 1, CP, stride=32), token_row(s, 1))
        return 0

    lax.fori_loop(1, 16, rows_of, 0)

    @pl.when(at_top)
    def _():
        g_mirror.wait()
        at = pl.ds(31, CP, stride=32)
        put(sbuf, at, get(sbuf, at) + dot(rfold[...], fold_sel[...]))

    stores = []
    outs = [(xs_out, 0, 0, SC * 32)]
    for k in range(6):
        outs.append((xf_out, k * 512, F0 * 32 + k * 512, 512))
    for n, (dst, at, to, rows) in enumerate(outs):
        cells = dot(get(sbuf, pl.ds(to, rows)).astype(BF16), permt[...]).astype(BF16)
        cells = cells.reshape(rows // 32, 32, 512) * mask_bf[None]
        raw[pl.ds(to, rows), :] = cells.reshape(rows, 512)
        copy = pltpu.make_async_copy(raw.at[pl.ds(to, rows)], dst.at[pl.ds(at, rows)], out_sem.at[n])
        copy.start()
        stores.append(copy)
    for copy in stores:
        copy.wait()
    g_copy.wait()


def on_device(state, forcing, land_mask, partner, cotangent, weight_state, weight_force):
    sc, fc = state.shape[1], forcing.shape[1]
    rows, cols = state.shape[2:]
    width = cotangent.shape[1]
    lon_n, lat_n, batch_n = (lax.axis_size(a) for a in ("lon", "lat", "batch"))
    local_col = (partner - (lon_n - 1 - lax.axis_index("lon")) * cols)[None, :]
    any_spec = pl.BlockSpec(memory_space=pl.ANY)
    vmem = pl.BlockSpec(memory_space=pltpu.VMEM)
    g, xs, xf = pl.pallas_call(
        main_kernel,
        out_shape=(
            jax.ShapeDtypeStruct((8, width, 256), F32),
            jax.ShapeDtypeStruct((sc * rows, cols), BF16),
            jax.ShapeDtypeStruct((fc * rows, cols), BF16),
        ),
        in_specs=[any_spec, any_spec, vmem, vmem, any_spec, any_spec, any_spec],
        out_specs=(any_spec, any_spec, any_spec),
        scratch_shapes=[
            pltpu.VMEM((4096, 512), BF16),
            pltpu.VMEM((4, 4096, 128), F32),
            pltpu.VMEM((8 * CP, 17 * 256), BF16),
            pltpu.VMEM((8192, 256), BF16),
            pltpu.VMEM((2, 8192, 128), F32),
            pltpu.VMEM((512, 4096), BF16),
            pltpu.VMEM((18 * 512, 256), BF16),
            pltpu.VMEM((1024, 1024), BF16),
            pltpu.VMEM((8, 512, 256), F32),
            pltpu.VMEM((512, 1536), BF16),
            pltpu.VMEM((384, 512), BF16),
            pltpu.VMEM((512, 512), BF16),
            pltpu.VMEM((512, 512), BF16),
            pltpu.VMEM((512, 512), BF16),
            pltpu.VMEM((512, 256), BF16),
            pltpu.VMEM((512, 256), BF16),
            pltpu.VMEM((256, 256), BF16),
            pltpu.VMEM((512, 256), BF16),
            pltpu.VMEM((512, 256), BF16),
            pltpu.VMEM((CP, 128), BF16),
            pltpu.VMEM((CP, 128), BF16),
            pltpu.VMEM((CP, 128), BF16),
            pltpu.VMEM((512, 128), BF16),
            pltpu.VMEM((512, 128), BF16),
            pltpu.VMEM((512, 128), BF16),
            pltpu.VMEM((CP, 512), BF16),
            pltpu.VMEM((CP, 512), BF16),
            pltpu.SemaphoreType.DMA((10,)),
            pltpu.SemaphoreType.DMA((9,)),
            pltpu.SemaphoreType.DMA((10,)),
            pltpu.SemaphoreType.DMA((10,)),
        ],
        compiler_params=pltpu.CompilerParams(
            collective_id=0, has_side_effects=True, vmem_limit_bytes=62 * 1024 * 1024
        ),
        name="encoder_backward",
    )(
        state.reshape(sc * rows, cols), forcing.reshape(fc * rows, cols), land_mask, local_col,
        cotangent.reshape(width * cotangent.shape[2], cotangent.shape[3]), weight_state.T, weight_force,
    )
    scale = 1.0 / math.sqrt(batch_n * (rows // 2) * lat_n * (cols // 2) * lon_n)
    share = lax.psum_scatter(g, ("lat", "batch"), scatter_dimension=1, tiled=True)
    share = lax.psum(share, "lon") * scale
    own = share.shape[1]
    share = share.reshape(2, 4, own, 2, CP)
    offsets = []
    for i in range(4):
        n = [r[0] for r in ROWS].index(i)
        for j in range(4):
            k = JORD.index(j)
            offsets.append(share[k // 2, n, :, k % 2, :])
    kernel = jnp.stack(offsets, axis=-1)
    return (
        xs.reshape(state.shape),
        xf.reshape(forcing.shape),
        kernel[:, :sc].reshape(own, sc * 16),
        kernel[:, F0:F0 + fc].reshape(own, fc * 16),
    )


def solution(mesh):
    in_specs = (
        P("batch", None, "lat", "lon"),
        P("batch", None, "lat", "lon"),
        P("lat", "lon"),
        P("lon"),
        P("batch", None, "lat", "lon"),
        P(),
        P(),
    )
    out_specs = (
        P("batch", None, "lat", "lon"),
        P("batch", None, "lat", "lon"),
        P(("lat", "batch"), None),
        P(("lat", "batch"), None),
    )
    return jax.shard_map(on_device, mesh=mesh, in_specs=in_specs, out_specs=out_specs, check_vma=False)
```

time: 754 us -> 281 us (0.37); the launches traced: 741 us -> 280 us
  local copies, waits for them, and re-layouts: 495 us -> 14.6 us
  waiting for transfers between devices: 102 us -> 181 us
  Pallas kernels: 0 us -> 67.2 us
  other arithmetic: 63.3 us -> 2.94 us
  matrix products: 43.5 us -> 0 us
  starting transfers between devices: 22.2 us -> 0.08 us
    slice x20 -> x3, local copies, waits for them, and re-layouts: 271 us -> 3.89 us  [the longest x2 3.02 us: on_device(): kernel[:, F0:F0 + fc].reshape(own, fc * 16)]
    unnamed x70 -> x6, local copies, waits for them, and re-layouts: 120 us -> 7.38 us
    reduce_scatter x0 -> x1, waiting for transfers between devices: none -> 94.9 us  [on_device(): lax.psum_scatter(g, ('lat', 'batch'), scatter_dimension=1, tiled=True)]
    pallas_call x0 -> x1, Pallas kernels: none -> 67.2 us  [on_device(): pl.pallas_call(main_kernel, out_shape=(jax.ShapeDtypeStruct((8, width, 25...]
    reshape x1, local copies, waits for them, and re-layouts: 58.6 us -> 1.23 us  [on_device(): share = share.reshape(2, 4, own, 2, CP)]
    dot_general x17 -> x0, matrix products: 43.5 us -> none  [the longest x1 22.9 us: on_device(): lax.dot_general(weights, grad_ext, (((0,), (0,)), ((), ())), preferred_el...]
    another operation x18 -> x2, local copies, waits for them, and re-layouts: 32.5 us -> 2.05 us  [on_device(): kernel = jnp.stack(offsets, axis=-1)]
    ppermute x14 -> x0, starting transfers between devices: 22.2 us -> none  [the longest x6 10.5 us: partner_2(): return lax.ppermute(block, axis, route)]
  transfers between devices with their start and end apart: 15 -> 2, of which waited for: 3 -> 2; matrix products, arithmetic and copies ran while one was open for 79% -> 0% of each run, Pallas kernels for 0% -> 0%
where the time goes in v1:
time: 281 us; the launch traced here: 280 us
  waiting for transfers between devices  181 us (64%)
  Pallas kernels  67.2 us (24%)
  local copies, waits for them, and re-layouts  14.6 us (5%)
  between operations  14.1 us (5%)
  other arithmetic  2.94 us (1%)
    reduce_scatter x1, waiting for transfers between devices, on_device(): lax.psum_scatter(g, ('lat', 'batch'), scatter_dimension=1, tiled=True)  94.9 us
    psum x1, waiting for transfers between devices, on_device(): share = lax.psum(share, 'lon') * scale  86.4 us
    pallas_call x1, Pallas kernels, on_device(): pl.pallas_call(main_kernel, out_shape=(jax.ShapeDtypeStruct((8, width, 25...  67.2 us
    unnamed x6, local copies, waits for them, and re-layouts  7.38 us
  transfers between devices with their start and end apart: 2, of which 2 were waited for; matrix products, arithmetic and copies ran while one was open for 0% of the time, Pallas kernels for 0%

profile of v1, /device:TPU:0, one launch (start us, length us, event | category | flops | bytes accessed | tf_op | source)
XLA Modules:
  0.0 280.2 jit_solution(4014678964916888035)
XLA Ops:
  7.2 0.0 reduce-scatter.2.cloned.1.call-start
  7.2 1.3 broadcast_subtract_fusion
  8.5 67.2 %encoder_backward.1 = (f32[8,512,256]{2,1,0:T(8,128)}, bf16[672,512]{1,0:T(8,128)(2,1)}, bf16[3072,512]{1,0:T(8,128)(2,1)}) custom-call(bf16[672,512]{1,0:T(8,128)(2,1)} %bitcast.81, bf16[3072,512]{1,0:T(8,128)(2,1)} %bitcast.76, s32[32,512]{1,0:T(8,128)} %mask.1, s32[1,512]{1,0:T(1,128)} %bitcast.83, bf16[8192,256]{1,0:T(8,128)(2,1)} %bitcast.74, ...), custom_call_target="tpu_custom_call" | custom-call | tf_op jit(solution)/shard_map/encoder_backward/pallas_call | solution.py:323
  75.7 0.0 reduce-scatter.2.cloned.1.call-update
  75.8 0.0 all-reduce.2.cloned.1.call-start
  75.8 94.9 %reduce-scatter.2.cloned.1.call-done = f32[8,32,256]{2,1,0:T(8,128)} async-done(((f32[8,512,256]{2,1,0:T(8,128)}), f32[8,32,256]{2,1,0:T(8,128)}) %reduce-scatter.2.cloned.1.call-update) | async-done | bytes 262160 | tf_op jit(solution)/shard_map/reduce_scatter | solution.py:374
  170.7 0.0 all-reduce.2.cloned.1.call-update
  170.8 86.4 %all-reduce.2.cloned.1.call-done = f32[8,32,256]{2,1,0:T(8,128)} async-done(((f32[8,32,256]{2,1,0:T(8,128)}), f32[8,32,256]{2,1,0:T(8,128)}) %all-reduce.2.cloned.1.call-update) | async-done | bytes 262160 | tf_op jit(solution)/shard_map/psum | solution.py:375
  257.2 1.7 broadcast_multiply_fusion
  258.8 0.0 copy-start
  258.8 1.2 reshape.37
  260.1 0.9 slice_bitcast_fusion
  260.9 1.2 stack.3
  262.1 0.8 slice.89
  263.0 2.2 copy.63
  265.1 2.1 copy.65
  267.2 0.9 copy.62
  268.1 1.6 copy.64
  269.7 2.0 copy.85
  271.7 0.0 copy-done
  271.7 1.7 copy.86
Async XLA Ops:
  7.2 163.6 %reduce-scatter.2.cloned.1.call-start = ((), (), s32[]{:S(2)}) async-start(), calls=%async_computation.1 | async-start | bytes 4456448 | tf_op jit(solution)/shard_map/reduce_scatter | solution.py:374
  75.8 181.4 %all-reduce.2.cloned.1.call-start = ((), (), s32[]{:S(2)}) async-start(), calls=%async_computation.2 | async-start | bytes 524288 | tf_op jit(solution)/shard_map/psum | solution.py:375
  258.8 12.9 %copy-start = (bf16[3072,512]{1,0:T(8,128)(2,1)S(1)}, bf16[3072,512]{1,0:T(8,128)(2,1)}, u32[]{:S(2)}) copy-start(bf16[3072,512]{1,0:T(8,128)(2,1)} %get-tuple-element.8) | copy-start | bytes 9437188
Sparse Core Ops, SparseCore 0:
  75.9 94.8 reduce-scatter.1
  173.2 83.9 all-reduce.1

commit v2 on v1

--- a/solution.py
+++ b/solution.py
@@ -40,10 +40,11 @@
 
 def main_kernel(
     state, force, mask, local_col, cot, wst, wf,
-    g_out, xs_out, xf_out,
+    ks_out, kf_out, xs_out, xf_out,
     raw, sbuf, planes, craw, cf32, cot_a, cot_b, wcat, gbuf, wstage, wspad, perm, permt, fold_sel,
     rxs, rxn, rmir, rcs, rcn, sx, rxw, rxe, sc, rcw, rce, sfold, rfold,
-    in_sem, out_sem, send, recv,
+    rcore, ra_z, ra_x, ra_y, s2_z, s2_x, s2_y, rb_z, rb_x, rb_y, s3_z, s3_x, s3_y, rc_z, rc_x, rc_y, s4, gathered, tbuf,
+    in_sem, out_sem, send, recv, core_s, core_r, a_s, a_r, b_s, b_r, c_s, c_r, g_s, g_r,
 ):
     lon_n = lax.axis_size("lon")
     lat_n = lax.axis_size("lat")
@@ -56,6 +57,24 @@
     east = {"lon": lax.rem(lon + 1, lon_n)}
     west = {"lon": lax.rem(lon + lon_n - 1, lon_n)}
     mirror = {"lon": lon_n - 1 - lon}
+    at_y, at_z, core = lax.rem(lon, 4), lax.div(lat, 2), lax.rem(lat, 2)
+    x_lo, x_hi = lax.axis_index("batch"), lax.div(lon, 4)
+    spot = {"x": 2 * x_hi + x_lo, "y": at_y, "z": at_z}
+    other_core = {"lat": 2 * at_z + 1 - core}
+
+    def peer_on(axis, place):
+        if axis == "z":
+            return {"lat": 2 * place + core}
+        if axis == "y":
+            return {"lon": 4 * x_hi + place}
+        return {"lon": 4 * lax.div(place, 2) + at_y, "batch": lax.rem(place, 2)}
+
+    def lon_peer(d):
+        return {"lon": lax.rem(lon + d, lon_n)}
+
+    peers = [north, south, mirror, other_core] + [lon_peer(d) for d in range(1, 8)]
+    for axis in "xyz":
+        peers += [peer_on(axis, lax.rem(spot[axis] + d, 4)) for d in range(1, 4)]
 
     cuts = [(state, 0, 0, SC * 32)]
     for k in range(6):
@@ -70,9 +89,9 @@
         copy.start()
 
     barrier = pltpu.get_barrier_semaphore()
-    for peer in (north, south, east, west, mirror):
+    for peer in peers:
         pl.semaphore_signal(barrier, inc=1, device_id=peer, device_id_type=pl.DeviceIdType.MESH)
-    pl.semaphore_wait(barrier, 5)
+    pl.semaphore_wait(barrier, len(peers))
 
     def remote(n, src, dst, peer):
         return pltpu.make_async_remote_copy(
@@ -156,13 +175,116 @@
     c_north.start()
     c_south.start()
 
+    orders = ("zxy", "xyz", "yzx")
+    recv_a, sum_2 = (ra_z, ra_x, ra_y), (s2_z, s2_x, s2_y)
+    recv_b, sum_3 = (rb_z, rb_x, rb_y), (s3_z, s3_x, s3_y)
+    recv_c = (rc_z, rc_x, rc_y)
+
+    def part(axis, place):
+        every = slice(None)
+        if axis == "z":
+            return (pl.ds(place, 1), every, every, every, every)
+        if axis == "y":
+            return (every, every, pl.ds(place, 1), every, every)
+        lanes = pl.ds(pl.multiple_of(lax.div(place, 2) * 128, 128), 128)
+        return (every, pl.ds(lax.rem(place, 2), 1), every, every, lanes)
+
+    def exchange(axis, src, dst, ss, rs):
+        copies = []
+        for d in range(1, 4):
+            place = lax.rem(spot[axis] + d, 4)
+            copies.append(pltpu.make_async_remote_copy(
+                src_ref=src(part(axis, place)), dst_ref=dst(d - 1), send_sem=ss(d - 1), recv_sem=rs(d - 1),
+                device_id=peer_on(axis, place), device_id_type=pl.DeviceIdType.MESH,
+            ))
+        return copies
+
+    def core_copy(p):
+        return pltpu.make_async_remote_copy(
+            src_ref=gbuf.at[p, :, 1 - core], dst_ref=rcore.at[p], send_sem=core_s.at[p], recv_sem=core_r.at[p],
+            device_id=other_core, device_id_type=pl.DeviceIdType.MESH,
+        )
+
+    def a_copies(p):
+        k, slot = p % 3, p // 3
+        return exchange(
+            orders[k][0], lambda at_part: rcore.at[(p,) + at_part], lambda d: recv_a[k].at[slot, d],
+            lambda d: a_s.at[p, d], lambda d: a_r.at[p, d],
+        )
+
+    def b_copies(k):
+        return exchange(
+            orders[k][1], lambda at_part: sum_2[k].at[(slice(None),) + at_part], lambda d: recv_b[k].at[d],
+            lambda d: b_s.at[k, d], lambda d: b_r.at[k, d],
+        )
+
+    def c_copies(k):
+        return exchange(
+            orders[k][2], lambda at_part: sum_3[k].at[(slice(None),) + at_part], lambda d: recv_c[k].at[d],
+            lambda d: c_s.at[k, d], lambda d: c_r.at[k, d],
+        )
+
+    def g_copies():
+        return [
+            pltpu.make_async_remote_copy(
+                src_ref=s4, dst_ref=gathered.at[lon], send_sem=g_s.at[d - 1], recv_sem=g_r.at[d - 1],
+                device_id=lon_peer(d), device_id_type=pl.DeviceIdType.MESH,
+            )
+            for d in range(1, 8)
+        ]
+
+    def core_start(p, value):
+        gbuf[p] = value.reshape(4, 2, 2, 4, 8, 256)
+        core_copy(p).start()
+
+    def a_start(p):
+        core_copy(p).wait()
+        rcore[p] = rcore[p] + gbuf[p, :, core]
+        for copy in a_copies(p):
+            copy.start()
+
+    def b_start():
+        for p in range(8):
+            k, slot = p % 3, p // 3
+            for copy in a_copies(p):
+                copy.wait()
+            own = rcore[(p,) + part(orders[k][0], spot[orders[k][0]])]
+            got = recv_a[k][slot]
+            sum_2[k][slot] = own + got[0] + got[1] + got[2]
+        for k in range(3):
+            for copy in b_copies(k):
+                copy.start()
+
+    def c_start():
+        for k in range(3):
+            for copy in b_copies(k):
+                copy.wait()
+            own = sum_2[k][(slice(None),) + part(orders[k][1], spot[orders[k][1]])]
+            got = recv_b[k][...]
+            sum_3[k][...] = own + got[0] + got[1] + got[2]
+            for copy in c_copies(k):
+                copy.start()
+
+    def g_start():
+        for k in range(3):
+            for copy in c_copies(k):
+                copy.wait()
+            own = sum_3[k][(slice(None),) + part(orders[k][2], spot[orders[k][2]])]
+            got = recv_c[k][...]
+            total = own + got[0] + got[1] + got[2]
+            for slot in range(total.shape[0]):
+                s4[slot * 3 + k] = total[slot, 0, 0, 0]
+        for copy in g_copies():
+            copy.start()
+
     def tile(n, pair):
         _, parity, off = ROWS[n]
         rows = planes[pl.ds((parity * 4 + pair * 2) * CP, 2 * CP), pl.ds(off * 256, 4096)]
         return dot_nt(cot_a[...], rows)
 
-    gbuf[0] = tile(0, 0)
-    gbuf[1] = tile(1, 0)
+    core_start(0, tile(0, 0))
+    core_start(1, tile(1, 0))
+    a_start(0)
 
     natural = jnp.where(row5 == local_col[...], 1.0, 0.0).astype(BF16)
     half = dot(natural, perm[...]).astype(BF16)
@@ -213,8 +335,10 @@
     c_east.start()
     c_west.start()
 
-    gbuf[2] = tile(2, 0)
-    gbuf[3] = tile(3, 0)
+    core_start(2, tile(2, 0))
+    a_start(1)
+    core_start(3, tile(3, 0))
+    a_start(2)
     x_east.wait()
     x_west.wait()
     side = jnp.concatenate(
@@ -227,9 +351,8 @@
         last = (lrow >= 65) & (lrow <= 80) & (lcol == 2 * lrow - 130 + i)
         spread = jnp.where(first | last, 1.0, 0.0).astype(BF16)
         moved = dot(sc[...], spread).astype(BF16)
-        gbuf[4 + n] = tile(n, 1) + dot_nt(moved, side)
-    g_copy = pltpu.make_async_copy(gbuf, g_out, out_sem.at[8])
-    g_copy.start()
+        core_start(4 + n, tile(n, 1) + dot_nt(moved, side))
+        a_start(3 + n)
 
     loads[8].wait()
     loads[9].wait()
@@ -251,6 +374,8 @@
                     sbuf, pl.ds((i * 4 + JORD[j]) * CP, CP)
                 ).astype(BF16)
 
+    a_start(7)
+
     c_east.wait()
     c_west.wait()
     z_west, z_east = [], []
@@ -286,6 +411,9 @@
     def rows_of(s, _):
         put(sbuf, pl.ds(2 * s, CP, stride=32), token_row(s, 0))
         put(sbuf, pl.ds(2 * s - 1, CP, stride=32), token_row(s, 1))
+        pl.when(s == 4)(b_start)
+        pl.when(s == 8)(c_start)
+        pl.when(s == 12)(g_start)
         return 0
 
     lax.fori_loop(1, 16, rows_of, 0)
@@ -307,9 +435,26 @@
         copy = pltpu.make_async_copy(raw.at[pl.ds(to, rows)], dst.at[pl.ds(at, rows)], out_sem.at[n])
         copy.start()
         stores.append(copy)
+
+    for copy in g_copies():
+        copy.wait()
+    gathered[lon] = s4[...]
+    scale = 1.0 / math.sqrt(lax.axis_size("batch") * 16 * lat_n * 256 * lon_n)
+    for p in range(8):
+        for which in range(2):
+            o = ROWS[p % 4][0] * 4 + JORD[p // 4 * 2 + which]
+            rows = [gathered[4 * which + y, p] for y in range(4)] + [jnp.zeros((96, 128), F32)]
+            tbuf[pl.ds(o, 128, stride=16), :] = jnp.transpose(jnp.concatenate(rows, axis=0) * scale)
+    for k in range(3):
+        block = jnp.transpose(tbuf[pl.ds(k * 128, 128), :])[:32]
+        if k < 2:
+            ks_out[:, pl.ds(k * 128, 128)] = block
+        else:
+            ks_out[:, pl.ds(256, 80)] = block[:, :80]
+    for k in range(12):
+        kf_out[:, pl.ds(k * 128, 128)] = jnp.transpose(tbuf[pl.ds((k + 3) * 128, 128), :])[:32]
     for copy in stores:
         copy.wait()
-    g_copy.wait()
 
 
 def on_device(state, forcing, land_mask, partner, cotangent, weight_state, weight_force):
@@ -320,15 +465,16 @@
     local_col = (partner - (lon_n - 1 - lax.axis_index("lon")) * cols)[None, :]
     any_spec = pl.BlockSpec(memory_space=pl.ANY)
     vmem = pl.BlockSpec(memory_space=pltpu.VMEM)
-    g, xs, xf = pl.pallas_call(
+    ks, kf, xs, xf = pl.pallas_call(
         main_kernel,
         out_shape=(
-            jax.ShapeDtypeStruct((8, width, 256), F32),
+            jax.ShapeDtypeStruct((width // (lat_n * batch_n), sc * 16), F32),
+            jax.ShapeDtypeStruct((width // (lat_n * batch_n), fc * 16), F32),
             jax.ShapeDtypeStruct((sc * rows, cols), BF16),
             jax.ShapeDtypeStruct((fc * rows, cols), BF16),
         ),
         in_specs=[any_spec, any_spec, vmem, vmem, any_spec, any_spec, any_spec],
-        out_specs=(any_spec, any_spec, any_spec),
+        out_specs=(vmem, vmem, any_spec, any_spec),
         scratch_shapes=[
             pltpu.VMEM((4096, 512), BF16),
             pltpu.VMEM((4, 4096, 128), F32),
@@ -338,7 +484,7 @@
             pltpu.VMEM((512, 4096), BF16),
             pltpu.VMEM((18 * 512, 256), BF16),
             pltpu.VMEM((1024, 1024), BF16),
-            pltpu.VMEM((8, 512, 256), F32),
+            pltpu.VMEM((8, 4, 2, 2, 4, 8, 256), F32),
             pltpu.VMEM((512, 1536), BF16),
             pltpu.VMEM((384, 512), BF16),
             pltpu.VMEM((512, 512), BF16),
@@ -357,10 +503,39 @@
             pltpu.VMEM((512, 128), BF16),
             pltpu.VMEM((CP, 512), BF16),
             pltpu.VMEM((CP, 512), BF16),
+            pltpu.VMEM((8, 4, 2, 4, 8, 256), F32),
+            pltpu.VMEM((3, 3, 1, 2, 4, 8, 256), F32),
+            pltpu.VMEM((3, 3, 4, 1, 4, 8, 128), F32),
+            pltpu.VMEM((2, 3, 4, 2, 1, 8, 256), F32),
+            pltpu.VMEM((3, 1, 2, 4, 8, 256), F32),
+            pltpu.VMEM((3, 4, 1, 4, 8, 128), F32),
+            pltpu.VMEM((2, 4, 2, 1, 8, 256), F32),
+            pltpu.VMEM((3, 3, 1, 1, 4, 8, 128), F32),
+            pltpu.VMEM((3, 3, 4, 1, 1, 8, 128), F32),
+            pltpu.VMEM((3, 2, 1, 2, 1, 8, 256), F32),
+            pltpu.VMEM((3, 1, 1, 4, 8, 128), F32),
+            pltpu.VMEM((3, 4, 1, 1, 8, 128), F32),
+            pltpu.VMEM((2, 1, 2, 1, 8, 256), F32),
+            pltpu.VMEM((3, 3, 1, 1, 1, 8, 128), F32),
+            pltpu.VMEM((3, 3, 1, 1, 1, 8, 128), F32),
+            pltpu.VMEM((3, 2, 1, 1, 1, 8, 128), F32),
+            pltpu.VMEM((8, 8, 128), F32),
+            pltpu.VMEM((8, 8, 8, 128), F32),
+            pltpu.VMEM((2048, 128), F32),
             pltpu.SemaphoreType.DMA((10,)),
-            pltpu.SemaphoreType.DMA((9,)),
+            pltpu.SemaphoreType.DMA((8,)),
             pltpu.SemaphoreType.DMA((10,)),
             pltpu.SemaphoreType.DMA((10,)),
+            pltpu.SemaphoreType.DMA((8,)),
+            pltpu.SemaphoreType.DMA((8,)),
+            pltpu.SemaphoreType.DMA((8, 3)),
+            pltpu.SemaphoreType.DMA((8, 3)),
+            pltpu.SemaphoreType.DMA((3, 3)),
+            pltpu.SemaphoreType.DMA((3, 3)),
+            pltpu.SemaphoreType.DMA((3, 3)),
+            pltpu.SemaphoreType.DMA((3, 3)),
+            pltpu.SemaphoreType.DMA((7,)),
+            pltpu.SemaphoreType.DMA((7,)),
         ],
         compiler_params=pltpu.CompilerParams(
             collective_id=0, has_side_effects=True, vmem_limit_bytes=62 * 1024 * 1024
@@ -370,23 +545,11 @@
         state.reshape(sc * rows, cols), forcing.reshape(fc * rows, cols), land_mask, local_col,
         cotangent.reshape(width * cotangent.shape[2], cotangent.shape[3]), weight_state.T, weight_force,
     )
-    scale = 1.0 / math.sqrt(batch_n * (rows // 2) * lat_n * (cols // 2) * lon_n)
-    share = lax.psum_scatter(g, ("lat", "batch"), scatter_dimension=1, tiled=True)
-    share = lax.psum(share, "lon") * scale
-    own = share.shape[1]
-    share = share.reshape(2, 4, own, 2, CP)
-    offsets = []
-    for i in range(4):
-        n = [r[0] for r in ROWS].index(i)
-        for j in range(4):
-            k = JORD.index(j)
-            offsets.append(share[k // 2, n, :, k % 2, :])
-    kernel = jnp.stack(offsets, axis=-1)
     return (
         xs.reshape(state.shape),
         xf.reshape(forcing.shape),
-        kernel[:, :sc].reshape(own, sc * 16),
-        kernel[:, F0:F0 + fc].reshape(own, fc * 16),
+        ks,
+        kf,
     )
 
 

time: 281 us -> 88.2 us (0.31)
  waiting for transfers between devices: 181 us -> 0 us
  between operations: 14.1 us -> 0.65 us
  Pallas kernels: 67.2 us -> 77.6 us
  local copies, waits for them, and re-layouts: 14.6 us -> 7.33 us
    reduce_scatter x1 -> x0, waiting for transfers between devices: 94.9 us -> none  [on_device(): lax.psum_scatter(g, ('lat', 'batch'), scatter_dimension=1, tiled=True)]
    psum x1 -> x0, waiting for transfers between devices: 86.4 us -> none  [on_device(): share = lax.psum(share, 'lon') * scale]
    pallas_call x1, Pallas kernels: 67.2 us -> 77.6 us  [on_device(): pl.pallas_call(main_kernel, out_shape=(jax.ShapeDtypeStruct((width // (la...]
    slice x3 -> x0, local copies, waits for them, and re-layouts: 3.89 us -> none  [the longest x2 3.02 us: on_device(): kernel[:, F0:F0 + fc].reshape(own, fc * 16)]
    unnamed x6 -> x8, local copies, waits for them, and re-layouts: 7.38 us -> 7.33 us
  transfers between devices with their start and end apart: 2 -> 0, of which waited for: 2 -> 0; matrix products, arithmetic and copies ran while one was open for 0% -> 0% of each run, Pallas kernels for 0% -> 0%
where the time goes in v2:
time: 88.2 us; the launch traced here: 86.8 us
  Pallas kernels  77.6 us (88%)
  local copies, waits for them, and re-layouts  7.33 us (8%)
  other arithmetic  1.26 us (1%)
    pallas_call x1, Pallas kernels, on_device(): pl.pallas_call(main_kernel, out_shape=(jax.ShapeDtypeStruct((width // (la...  77.6 us
    unnamed x8, local copies, waits for them, and re-layouts  7.33 us

profile of v2, /device:TPU:0, one launch (start us, length us, event | category | flops | bytes accessed | tf_op | source)
XLA Modules:
  0.0 86.8 jit_solution(8110480653134758299)
XLA Ops:
  0.6 1.3 %broadcast_subtract_fusion = s32[512]{0:T(512)} fusion(s32[512]{0:T(512)} %param.10, s32[]{:T(128)S(6)} %mul.3), kind=kLoop, calls=%fused_computation | loop fusion | flops 512 | bytes 4100 | tf_op jit(solution)/shard_map/sub | solution.py:465
  1.9 77.6 %encoder_backward.1 = (f32[32,336]{1,0:T(8,128)}, f32[32,1536]{1,0:T(8,128)}, bf16[672,512]{1,0:T(8,128)(2,1)}, bf16[3072,512]{1,0:T(8,128)(2,1)}) custom-call(bf16[672,512]{1,0:T(8,128)(2,1)} %bitcast.11, bf16[3072,512]{1,0:T(8,128)(2,1)} %bitcast.9, s32[32,512]{1,0:T(8,128)} %mask.1, s32[1,512]{1,0:T(1,128)} %bitcast.13, bf16[8192,256]{1,0:T(8,128)(2,1)} %bitcast.7, ...), custom_call_target="tpu_custom_call" | custom-call | tf_op jit(solution)/shard_map/encoder_backward/pallas_call | solution.py:468
  79.5 2.0 %copy.15 = bf16[1,21,32,512]{3,2,1,0:T(8,128)(2,1)} copy(bf16[1,21,32,512]{3,2,1,0:T(8,128)(2,1)} %bitcast.10) | data formatting | bytes 1376256
  81.5 0.0 copy-start.1
  81.5 0.0 copy-start
  81.5 4.0 %copy.16 = bf16[1,96,32,512]{3,2,1,0:T(8,128)(2,1)} copy(bf16[1,96,32,512]{3,2,1,0:T(8,128)(2,1)} %bitcast.8) | data formatting | bytes 6291456
  85.5 0.0 copy-done.1
  85.5 0.6 copy.17
  86.1 0.0 copy-done
  86.1 0.7 copy.18
Async XLA Ops:
  81.5 4.0 %copy-start.1 = (f32[32,336]{1,0:T(8,128)S(1)}, f32[32,336]{1,0:T(8,128)}, u32[]{:S(2)}) copy-start(f32[32,336]{1,0:T(8,128)} %get-tuple-element.18) | copy-start | bytes 129028
  81.5 4.6 %copy-start = (f32[32,1536]{1,0:T(8,128)S(1)}, f32[32,1536]{1,0:T(8,128)}, u32[]{:S(2)}) copy-start(f32[32,1536]{1,0:T(8,128)} %get-tuple-element.19) | copy-start | bytes 589828

commit v3 on v2

v3 whole, which is shorter than its diff:
```python
import functools
import math

import jax
import jax.numpy as jnp
from jax import lax
from jax.experimental import pallas as pl
from jax.experimental.pallas import tpu as pltpu
from jax.sharding import PartitionSpec as P

SC = 21
FC = 96
CP = 128
F32 = jnp.float32
BF16 = jnp.bfloat16
JORD = (1, 2, 0, 3)
ROWS = ((1, 0, 0), (2, 1, 1), (0, 1, 0), (3, 0, 1))


def iota(shape, dim):
    return lax.broadcasted_iota(jnp.int32, shape, dim)


def dot(a, b):
    return lax.dot_general(a, b, (((1,), (0,)), ((), ())), preferred_element_type=F32)


def dot_nt(a, b):
    return lax.dot_general(a, b, (((1,), (1,)), ((), ())), preferred_element_type=F32)


def flag(where):
    return jnp.where(where, 1.0, 0.0).astype(BF16)


def main_kernel(
    state, force, mask, partner, cot, wst, wf,
    share_out, rows_out,
    raw, planes, craw, cot_a, cot_b, wcat, wscr, gbuf, wstage, wspad, perm, permt, perm2, permt2, fold_sel, top_row,
    rxs, rxn, rmir, rcs, rcn, sx, rxw, rxe, sc, rcw, rce, sfold, rfold,
    rcore, ra_z, ra_x, ra_y, s2_z, s2_x, s2_y, rb_z, rb_x, rb_y, s3_z, s3_x, s3_y, rc_z, rc_x, rc_y, s4, gathered,
    in_sem, out_sem, send, recv, core_s, core_r, a_s, a_r, b_s, b_r, c_s, c_r, g_s, g_r,
):
    lon_n = lax.axis_size("lon")
    lat_n = lax.axis_size("lat")
    lon = lax.axis_index("lon")
    lat = lax.axis_index("lat")
    at_top = lat == lat_n - 1
    at_bottom = lat == 0
    north = {"lat": lax.rem(lat + 1, lat_n)}
    south = {"lat": lax.rem(lat + lat_n - 1, lat_n)}
    east = {"lon": lax.rem(lon + 1, lon_n)}
    west = {"lon": lax.rem(lon + lon_n - 1, lon_n)}
    mirror = {"lon": lon_n - 1 - lon}
    at_y, at_z, core = lax.rem(lon, 4), lax.div(lat, 2), lax.rem(lat, 2)
    x_lo, x_hi = lax.axis_index("batch"), lax.div(lon, 4)
    spot = {"x": 2 * x_hi + x_lo, "y": at_y, "z": at_z}
    other_core = {"lat": 2 * at_z + 1 - core}

    def peer_on(axis, place):
        if axis == "z":
            return {"lat": 2 * place + core}
        if axis == "y":
            return {"lon": 4 * x_hi + place}
        return {"lon": 4 * lax.div(place, 2) + at_y, "batch": lax.rem(place, 2)}

    def lon_peer(d):
        return {"lon": lax.rem(lon + d, lon_n)}

    peers = [north, south, mirror, other_core] + [lon_peer(d) for d in range(1, 8)]
    for axis in "xyz":
        peers += [peer_on(axis, lax.rem(spot[axis] + d, 4)) for d in range(1, 4)]

    loads = []
    for k in range(6):
        loads.append(pltpu.make_async_copy(force.at[pl.ds(k * 512, 512)], raw.at[pl.ds(k * 512, 512)], in_sem.at[k]))
    loads.append(pltpu.make_async_copy(state, raw.at[pl.ds(FC * 32, SC * 32)], in_sem.at[6]))
    loads.append(pltpu.make_async_copy(cot, craw, in_sem.at[7]))
    loads.append(pltpu.make_async_copy(wst, wspad.at[pl.ds(0, 336)], in_sem.at[8]))
    loads.append(pltpu.make_async_copy(wf, wstage, in_sem.at[9]))
    for copy in loads:
        copy.start()

    barrier = pltpu.get_barrier_semaphore()
    for peer in peers:
        pl.semaphore_signal(barrier, inc=1, device_id=peer, device_id_type=pl.DeviceIdType.MESH)
    def remote(n, src, dst, peer):
        return pltpu.make_async_remote_copy(
            src_ref=src, dst_ref=dst, send_sem=send.at[n], recv_sem=recv.at[n],
            device_id=peer, device_id_type=pl.DeviceIdType.MESH,
        )

    down, across = iota((512, 1), 0), iota((1, 512), 1)

    def column(lane, late):
        half = lax.shift_right_logical(lane, 8)
        return (2 * lane + (-half if late else half)) & 511

    perm[...] = flag(down == column(across, False))
    permt[...] = flag(column(down, False) == across)
    perm2[...] = flag(down == column(across, True))
    permt2[...] = flag(column(down, True) == across)

    raw[pl.ds((FC + SC) * 32, (CP - FC - SC) * 32), :] = jnp.zeros(((CP - FC - SC) * 32, 512), BF16)
    mask_bf = mask[...].astype(F32).astype(BF16)
    zero16 = jnp.zeros((), BF16)
    lane128 = iota((CP, 128), 1)

    def put_row(parity, slot, channels, both):
        n = both.shape[0]
        lane256 = iota((n, 256), 1)
        even, odd = both[:, :256], both[:, 256:]
        left = jnp.where(lane256 == 0, zero16, pltpu.roll(odd, 1, 1))
        right = jnp.where(lane256 == 255, zero16, pltpu.roll(even, 255, 1))
        for j, part in enumerate((even, odd, left, right)):
            planes[pl.ds((parity * 4 + j) * CP + channels, n), pl.ds(slot * 256, 256)] = part

    lane16 = iota((16, 128), 1)
    for k in range(8):
        if k < 7:
            loads[k].wait()
        x = raw[pl.ds(k * 512, 512), :].reshape(16, 32, 512) * mask_bf[None]
        y = dot(x.reshape(512, 512), perm[...]).astype(BF16)
        y = jnp.swapaxes(y.reshape(16, 32, 512), 0, 1)
        edge = jnp.zeros((16, 128), BF16)
        for r in range(32):
            put_row(r % 2, r // 2 + r % 2, k * 16, y[r])
            edge = jnp.where(lane16 == r + 1, y[r][:, 0:1], edge)
            edge = jnp.where(lane16 == 65 + r, y[r][:, 511:512], edge)
        sx[pl.ds(k * 16, 16), :] = edge

    pl.semaphore_wait(barrier, len(peers))
    x_north = remote(0, planes.at[pl.ds(512, 512), pl.ds(16 * 256, 256)], rxs, north)
    x_south = remote(1, planes.at[pl.ds(0, 512), pl.ds(0, 256)], rxn, south)
    x_mirror = remote(2, planes.at[pl.ds(512, 256), pl.ds(16 * 256, 256)], rmir, mirror)
    x_north.start()
    x_south.start()

    @pl.when(at_top)
    def _():
        x_mirror.start()

    loads[7].wait()
    clane = iota((512, 128), 1)
    lane32 = iota((32, 128), 1)

    def late(x):
        return jnp.where(iota(x.shape, 1) == 0, zero16, pltpu.roll(x, 1, 1))

    def split_tokens(k, _):
        x = craw[pl.ds(pl.multiple_of(k * 512, 512), 512), :].reshape(32, 16, 256)
        y = jnp.swapaxes(x, 0, 1)
        w = pl.multiple_of(k * 32, 32)
        edge = jnp.zeros((32, 128), BF16)
        for a in range(16):
            cot_a[pl.ds(w, 32), pl.ds(a * 256, 256)] = y[a]
            cot_b[pl.ds((a + 1) * 1024 + w, 32), :] = y[a]
            cot_b[pl.ds((a + 1) * 1024 + 512 + w, 32), :] = late(y[a])
            edge = jnp.where(lane32 == a + 1, y[a][:, 0:1], edge)
            edge = jnp.where(lane32 == 65 + a, y[a][:, 255:256], edge)
        sc[pl.ds(w, 32), :] = edge
        return 0

    lax.fori_loop(0, 16, split_tokens, 0)
    c_north = remote(3, cot_b.at[pl.ds(16 * 1024, 512)], rcs, north)
    c_south = remote(4, cot_b.at[pl.ds(1024, 512)], rcn, south)
    c_north.start()
    c_south.start()

    def tile(n, pair):
        _, parity, off = ROWS[n]
        rows = planes[pl.ds((parity * 4 + pair * 2) * CP, 2 * CP), pl.ds(off * 256, 4096)]
        return dot_nt(cot_a[...], rows)

    orders = ("zxy", "xyz", "yzx")
    recv_a, sum_2 = (ra_z, ra_x, ra_y), (s2_z, s2_x, s2_y)
    recv_b, sum_3 = (rb_z, rb_x, rb_y), (s3_z, s3_x, s3_y)
    recv_c = (rc_z, rc_x, rc_y)

    def part(axis, place):
        every = slice(None)
        if axis == "z":
            return (pl.ds(place, 1), every, every, every, every)
        if axis == "y":
            return (every, every, pl.ds(place, 1), every, every)
        lanes = pl.ds(pl.multiple_of(lax.div(place, 2) * 128, 128), 128)
        return (every, pl.ds(lax.rem(place, 2), 1), every, every, lanes)

    def exchange(axis, src, dst, ss, rs):
        copies = []
        for d in range(1, 4):
            place = lax.rem(spot[axis] + d, 4)
            copies.append(pltpu.make_async_remote_copy(
                src_ref=src(part(axis, place)), dst_ref=dst(d - 1), send_sem=ss(d - 1), recv_sem=rs(d - 1),
                device_id=peer_on(axis, place), device_id_type=pl.DeviceIdType.MESH,
            ))
        return copies

    def core_copy(p):
        return pltpu.make_async_remote_copy(
            src_ref=gbuf.at[p, :, 1 - core], dst_ref=rcore.at[p], send_sem=core_s.at[p], recv_sem=core_r.at[p],
            device_id=other_core, device_id_type=pl.DeviceIdType.MESH,
        )

    def a_copies(p):
        k, slot = p % 3, p // 3
        return exchange(
            orders[k][0], lambda at_part: rcore.at[(p,) + at_part], lambda d: recv_a[k].at[slot, d],
            lambda d: a_s.at[p, d], lambda d: a_r.at[p, d],
        )

    def b_copies(k):
        return exchange(
            orders[k][1], lambda at_part: sum_2[k].at[(slice(None),) + at_part], lambda d: recv_b[k].at[d],
            lambda d: b_s.at[k, d], lambda d: b_r.at[k, d],
        )

    def c_copies(k):
        return exchange(
            orders[k][2], lambda at_part: sum_3[k].at[(slice(None),) + at_part], lambda d: recv_c[k].at[d],
            lambda d: c_s.at[k, d], lambda d: c_r.at[k, d],
        )

    def g_copies():
        return [
            pltpu.make_async_remote_copy(
                src_ref=s4, dst_ref=gathered.at[lon], send_sem=g_s.at[d - 1], recv_sem=g_r.at[d - 1],
                device_id=lon_peer(d), device_id_type=pl.DeviceIdType.MESH,
            )
            for d in range(1, 8)
        ]

    def core_start(p, value):
        gbuf[p] = value.reshape(4, 2, 2, 4, 8, 256)
        core_copy(p).start()

    def a_start(p):
        core_copy(p).wait()
        rcore[p] = rcore[p] + gbuf[p, :, core]
        for copy in a_copies(p):
            copy.start()

    def b_start():
        for p in range(8):
            k, slot = p % 3, p // 3
            for copy in a_copies(p):
                copy.wait()
            own = rcore[(p,) + part(orders[k][0], spot[orders[k][0]])]
            got = recv_a[k][slot]
            sum_2[k][slot] = own + got[0] + got[1] + got[2]
        for k in range(3):
            for copy in b_copies(k):
                copy.start()

    def c_start():
        for k in range(3):
            for copy in b_copies(k):
                copy.wait()
            own = sum_2[k][(slice(None),) + part(orders[k][1], spot[orders[k][1]])]
            got = recv_b[k][...]
            sum_3[k][...] = own + got[0] + got[1] + got[2]
            for copy in c_copies(k):
                copy.start()

    def g_start():
        for k in range(3):
            for copy in c_copies(k):
                copy.wait()
            own = sum_3[k][(slice(None),) + part(orders[k][2], spot[orders[k][2]])]
            got = recv_c[k][...]
            total = own + got[0] + got[1] + got[2]
            for slot in range(total.shape[0]):
                s4[slot * 3 + k] = total[slot, 0, 0, 0]
        for copy in g_copies():
            copy.start()

    def tile(n, pair):
        _, parity, off = ROWS[n]
        rows = planes[pl.ds((parity * 4 + pair * 2) * CP, 2 * CP), pl.ds(off * 256, 4096)]
        return dot_nt(cot_a[...], rows)

    core_start(0, tile(0, 0))
    core_start(1, tile(1, 0))
    a_start(0)

    fold_sel[...] = flag(down == partner[...] - (lon_n - 1 - lon) * 512)

    def folded(x, before, after):
        x = dot(x, before[...]).astype(BF16)
        x = dot(x, fold_sel[...]).astype(BF16)
        return dot(x, after[...])

    x_north.wait()
    x_south.wait()
    planes[pl.ds(512, 512), pl.ds(0, 256)] = jnp.where(at_bottom, zero16, rxs[...])
    planes[pl.ds(0, 512), pl.ds(16 * 256, 256)] = rxn[...]

    @pl.when(at_top)
    def _():
        x_mirror.wait()
        top = jnp.concatenate([rmir[pl.ds(0, CP), :], rmir[pl.ds(CP, CP), :]], axis=1)
        put_row(0, 16, 0, folded(top, permt, perm).astype(BF16))

    acc = sx[...]
    acc = jnp.where(lane128 == 0, planes[pl.ds(512, CP), pl.ds(0, 128)][:, 0:1], acc)
    acc = jnp.where(lane128 == 64, planes[pl.ds(512 + CP, CP), pl.ds(128, 128)][:, 127:128], acc)
    acc = jnp.where(lane128 == 33, planes[pl.ds(0, CP), pl.ds(16 * 256, 128)][:, 0:1], acc)
    acc = jnp.where(lane128 == 97, planes[pl.ds(CP, CP), pl.ds(16 * 256 + 128, 128)][:, 127:128], acc)
    sx[...] = acc
    x_east = remote(5, sx, rxw, east)
    x_west = remote(6, sx, rxe, west)
    x_east.start()
    x_west.start()

    c_north.wait()
    c_south.wait()
    low = jnp.where(at_bottom, zero16, rcs[...])
    high = jnp.where(at_top, zero16, rcn[...])
    for slot, x in ((0, low), (17, high)):
        cot_b[pl.ds(slot * 1024, 512), :] = x
        cot_b[pl.ds(slot * 1024 + 512, 512), :] = late(x)
    acc = sc[...]
    acc = jnp.where(clane == 0, low[:, 0:1], acc)
    acc = jnp.where(clane == 64, low[:, 255:256], acc)
    acc = jnp.where(clane == 17, high[:, 0:1], acc)
    acc = jnp.where(clane == 81, high[:, 255:256], acc)
    sc[...] = acc
    c_east = remote(7, sc, rcw, east)
    c_west = remote(8, sc, rce, west)
    c_east.start()
    c_west.start()

    core_start(2, tile(2, 0))
    a_start(1)
    core_start(3, tile(3, 0))
    a_start(2)
    x_east.wait()
    x_west.wait()
    side = jnp.concatenate(
        [jnp.where(lane128 >= 64, rxw[...], zero16), jnp.where(lane128 < 64, rxe[...], zero16)], axis=0
    )
    lrow, lcol = iota((128, 128), 0), iota((128, 128), 1)
    for n in range(4):
        i = ROWS[n][0]
        first = (lrow >= 1) & (lrow <= 16) & (lcol == 62 + 2 * lrow + i)
        last = (lrow >= 65) & (lrow <= 80) & (lcol == 2 * lrow - 130 + i)
        spread = jnp.where(first | last, 1.0, 0.0).astype(BF16)
        moved = dot(sc[...], spread).astype(BF16)
        core_start(4 + n, tile(n, 1) + dot_nt(moved, side))
        a_start(3 + n)

    loads[8].wait()
    loads[9].wait()
    wspad[pl.ds(336, 48), :] = jnp.zeros((48, 512), BF16)
    pick = flag((lrow & 7) * 16 + lax.shift_right_logical(lrow, 3) == lcol)
    for o in range(16):
        wscr[pl.ds(o * CP + 120, 8), :] = jnp.zeros((8, 512), F32)
    for kb in range(15):
        if kb < 12:
            got = dot_nt(pick, wstage[:, pl.ds(kb * 128, 128)])
        else:
            got = dot(pick, wspad[pl.ds((kb - 12) * 128, 128), :])
        for o in range(16):
            wscr[pl.ds(o * CP + kb * 8, 8), :] = got[o * 8:o * 8 + 8, :]
    for parity in range(2):
        for q in range(2):
            for n, i in enumerate(((3, 1), (2, 0))[parity]):
                for m, j in enumerate(((1, 3), (0, 2))[q]):
                    wcat[pl.ds((parity * 2 + q) * CP, CP), pl.ds((n * 2 + m) * 512, 512)] = wscr[
                        pl.ds((i * 4 + j) * CP, CP), :
                    ].astype(BF16)
    a_start(7)

    c_east.wait()
    c_west.wait()
    for slot in range(18):
        at = (pl.ds(slot * 1024 + 512, 512), pl.ds(0, 128))
        cot_b[at] = jnp.where(clane == 0, rcw[...][:, 64 + slot:65 + slot], cot_b[at])
    last = []
    for parity in range(2):
        w_rows = wcat[pl.ds((parity * 2 + 1) * CP, CP), :]
        total = dot(w_rows[:, :512], rce[...]) + pltpu.roll(dot(w_rows[:, 512:1024], sc[...]), 64, 1)
        total = total + pltpu.roll(dot(w_rows[:, 1024:1536], rce[...]), 127, 1)
        last.append(total + pltpu.roll(dot(w_rows[:, 1536:], sc[...]), 63, 1))

    def token_row(s, parities):
        tokens = cot_b[pl.ds(pl.multiple_of(s * 1024, 1024), 2048), :]
        u = dot(wcat[pl.ds(0, 256 * parities), :], tokens)
        rows = []
        for parity in range(parities):
            even, odd = u[parity * 256:parity * 256 + 128], u[parity * 256 + 128:parity * 256 + 256]
            first = jnp.where(lane128 == 0, pltpu.roll(last[parity], lax.rem(128 - s, 128), 1), odd[:, :128])
            rows.append(jnp.concatenate([even, first, odd[:, 128:]], axis=1))
        return rows

    fold, top = token_row(16, 2)
    sfold[...] = fold.astype(BF16)
    top_row[...] = top
    g_mirror = remote(9, sfold, rfold, mirror)

    @pl.when(at_top)
    def _():
        g_mirror.start()

    raw[pl.ds(0, CP), :] = token_row(0, 1)[0].astype(BF16)

    def out_copy(n, first, count):
        return pltpu.make_async_copy(raw.at[pl.ds(first * CP, count * CP)], rows_out.at[pl.ds(first * CP, count * CP)], out_sem.at[n])

    def rows_of(s, _):
        even, odd = token_row(s, 2)
        raw[pl.ds(pl.multiple_of(2 * s * CP, CP), CP), :] = even.astype(BF16)
        raw[pl.ds(pl.multiple_of((2 * s - 1) * CP, CP), CP), :] = odd.astype(BF16)
        pl.when(s == 4)(b_start)
        pl.when(s == 8)(c_start)
        pl.when(s == 9)(lambda: out_copy(0, 0, 19).start())
        pl.when(s == 12)(g_start)
        return 0

    lax.fori_loop(1, 16, rows_of, 0)
    out_copy(1, 19, 12).start()

    @pl.when(at_top)
    def _():
        g_mirror.wait()
        top_row[...] = top_row[...] + folded(rfold[...], permt2, perm2)

    raw[pl.ds(31 * CP, CP), :] = top_row[...].astype(BF16)
    out_copy(2, 31, 1).start()
    for copy in g_copies():
        copy.wait()
    gathered[lon] = s4[...]
    out_share = pltpu.make_async_copy(gathered, share_out, out_sem.at[3])
    out_share.start()
    for n, first, count in ((0, 0, 19), (1, 19, 12), (2, 31, 1)):
        out_copy(n, first, count).wait()
    out_share.wait()


def last_kernel(scale, share, rows, mask, ks_out, kf_out, xs_out, xf_out, permt2):
    k = pl.program_id(0)

    @pl.when(k == 0)
    def _():
        lane, across = iota((512, 1), 0), iota((1, 512), 1)
        permt2[...] = flag(((2 * lane - lax.shift_right_logical(lane, 8)) & 511) == across)
        turned = [None] * 16
        for p in range(8):
            for which in range(2):
                o = ROWS[p % 4][0] * 4 + JORD[p // 4 * 2 + which]
                own = [share[4 * which + y, p] for y in range(4)] + [jnp.zeros((96, 128), F32)]
                turned[o] = jnp.transpose(jnp.concatenate(own, axis=0)) * scale
        for n in range(15):
            block = jnp.stack([x[n * 8:n * 8 + 8] for x in turned], axis=0)
            block = jnp.transpose(jnp.swapaxes(block, 0, 1).reshape(128, 128))[:32]
            if n < 12:
                kf_out[:, pl.ds(n * 128, 128)] = block
            elif n < 14:
                ks_out[:, pl.ds((n - 12) * 128, 128)] = block
            else:
                ks_out[:, pl.ds(256, 80)] = block[:, :80]

    x = jnp.swapaxes(rows[...], 0, 1).reshape(512, 512)
    cells = dot(x, permt2[...]).astype(BF16).reshape(16, 32, 512)
    cells = (cells * mask[...].astype(F32).astype(BF16)[None]).reshape(512, 512)

    @pl.when(k < 6)
    def _():
        xf_out[...] = cells

    @pl.when(k >= 6)
    def _():
        xs_out[...] = cells


def on_device(state, forcing, land_mask, partner, cotangent, weight_state, weight_force):
    sc, fc = state.shape[1], forcing.shape[1]
    rows, cols = state.shape[2:]
    width = cotangent.shape[1]
    lon_n, lat_n, batch_n = (lax.axis_size(a) for a in ("lon", "lat", "batch"))
    any_spec = pl.BlockSpec(memory_space=pl.ANY)
    vmem = pl.BlockSpec(memory_space=pltpu.VMEM)
    share, cells = pl.pallas_call(
        main_kernel,
        out_shape=(
            jax.ShapeDtypeStruct((8, 8, 8, 128), F32),
            jax.ShapeDtypeStruct((rows * CP, cols), BF16),
        ),
        in_specs=[any_spec, any_spec, vmem, vmem, any_spec, any_spec, any_spec],
        out_specs=(any_spec, any_spec),
        scratch_shapes=[
            pltpu.VMEM((4096, 512), BF16),
            pltpu.VMEM((8 * CP, 17 * 256), BF16),
            pltpu.VMEM((8192, 256), BF16),
            pltpu.VMEM((512, 4096), BF16),
            pltpu.VMEM((18 * 1024, 256), BF16),
            pltpu.VMEM((512, 2048), BF16),
            pltpu.VMEM((2048, 512), F32),
            pltpu.VMEM((8, 4, 2, 2, 4, 8, 256), F32),
            pltpu.VMEM((512, 1536), BF16),
            pltpu.VMEM((384, 512), BF16),
            pltpu.VMEM((512, 512), BF16),
            pltpu.VMEM((512, 512), BF16),
            pltpu.VMEM((512, 512), BF16),
            pltpu.VMEM((512, 512), BF16),
            pltpu.VMEM((512, 512), BF16),
            pltpu.VMEM((CP, 512), F32),
            pltpu.VMEM((512, 256), BF16),
            pltpu.VMEM((512, 256), BF16),
            pltpu.VMEM((256, 256), BF16),
            pltpu.VMEM((512, 256), BF16),
            pltpu.VMEM((512, 256), BF16),
            pltpu.VMEM((CP, 128), BF16),
            pltpu.VMEM((CP, 128), BF16),
            pltpu.VMEM((CP, 128), BF16),
            pltpu.VMEM((512, 128), BF16),
            pltpu.VMEM((512, 128), BF16),
            pltpu.VMEM((512, 128), BF16),
            pltpu.VMEM((CP, 512), BF16),
            pltpu.VMEM((CP, 512), BF16),
            pltpu.VMEM((8, 4, 2, 4, 8, 256), F32),
            pltpu.VMEM((3, 3, 1, 2, 4, 8, 256), F32),
            pltpu.VMEM((3, 3, 4, 1, 4, 8, 128), F32),
            pltpu.VMEM((2, 3, 4, 2, 1, 8, 256), F32),
            pltpu.VMEM((3, 1, 2, 4, 8, 256), F32),
            pltpu.VMEM((3, 4, 1, 4, 8, 128), F32),
            pltpu.VMEM((2, 4, 2, 1, 8, 256), F32),
            pltpu.VMEM((3, 3, 1, 1, 4, 8, 128), F32),
            pltpu.VMEM((3, 3, 4, 1, 1, 8, 128), F32),
            pltpu.VMEM((3, 2, 1, 2, 1, 8, 256), F32),
            pltpu.VMEM((3, 1, 1, 4, 8, 128), F32),
            pltpu.VMEM((3, 4, 1, 1, 8, 128), F32),
            pltpu.VMEM((2, 1, 2, 1, 8, 256), F32),
            pltpu.VMEM((3, 3, 1, 1, 1, 8, 128), F32),
            pltpu.VMEM((3, 3, 1, 1, 1, 8, 128), F32),
            pltpu.VMEM((3, 2, 1, 1, 1, 8, 128), F32),
            pltpu.VMEM((8, 8, 128), F32),
            pltpu.VMEM((8, 8, 8, 128), F32),
            pltpu.SemaphoreType.DMA((10,)),
            pltpu.SemaphoreType.DMA((8,)),
            pltpu.SemaphoreType.DMA((10,)),
            pltpu.SemaphoreType.DMA((10,)),
            pltpu.SemaphoreType.DMA((8,)),
            pltpu.SemaphoreType.DMA((8,)),
            pltpu.SemaphoreType.DMA((8, 3)),
            pltpu.SemaphoreType.DMA((8, 3)),
            pltpu.SemaphoreType.DMA((3, 3)),
            pltpu.SemaphoreType.DMA((3, 3)),
            pltpu.SemaphoreType.DMA((3, 3)),
            pltpu.SemaphoreType.DMA((3, 3)),
            pltpu.SemaphoreType.DMA((7,)),
            pltpu.SemaphoreType.DMA((7,)),
        ],
        compiler_params=pltpu.CompilerParams(
            collective_id=0, has_side_effects=True, vmem_limit_bytes=62 * 1024 * 1024
        ),
        name="encoder_backward",
    )(
        state.reshape(sc * rows, cols), forcing.reshape(fc * rows, cols), land_mask, partner[None, :],
        cotangent.reshape(width * cotangent.shape[2], cotangent.shape[3]), weight_state.T, weight_force,
    )
    scale = 1.0 / math.sqrt(batch_n * (rows // 2) * lat_n * (cols // 2) * lon_n)
    own = width // (lat_n * batch_n)
    ks, kf, xs, xf = pl.pallas_call(
        functools.partial(last_kernel, scale),
        grid=(8,),
        out_shape=(
            jax.ShapeDtypeStruct((own, sc * 16), F32),
            jax.ShapeDtypeStruct((own, fc * 16), F32),
            jax.ShapeDtypeStruct((sc * rows, cols), BF16),
            jax.ShapeDtypeStruct((fc * rows, cols), BF16),
        ),
        in_specs=[
            pl.BlockSpec((8, 8, 8, 128), lambda k: (0, 0, 0, 0)),
            pl.BlockSpec((rows, 16, cols), lambda k: (0, k, 0)),
            pl.BlockSpec((rows, cols), lambda k: (0, 0)),
        ],
        out_specs=(
            pl.BlockSpec((own, sc * 16), lambda k: (0, 0)),
            pl.BlockSpec((own, fc * 16), lambda k: (0, 0)),
            pl.BlockSpec((16 * rows, cols), lambda k: (jnp.maximum(k - 6, 0), 0)),
            pl.BlockSpec((16 * rows, cols), lambda k: (jnp.minimum(k, 5), 0)),
        ),
        scratch_shapes=[pltpu.VMEM((512, 512), BF16)],
        name="encoder_finish",
    )(share, cells.reshape(rows, CP, cols), land_mask)
    return (
        xs.reshape(state.shape),
        xf.reshape(forcing.shape),
        ks,
        kf,
    )


def solution(mesh):
    in_specs = (
        P("batch", None, "lat", "lon"),
        P("batch", None, "lat", "lon"),
        P("lat", "lon"),
        P("lon"),
        P("batch", None, "lat", "lon"),
        P(),
        P(),
    )
    out_specs = (
        P("batch", None, "lat", "lon"),
        P("batch", None, "lat", "lon"),
        P(("lat", "batch"), None),
        P(("lat", "batch"), None),
    )
    return jax.shard_map(on_device, mesh=mesh, in_specs=in_specs, out_specs=out_specs, check_vma=False)
```

time: 88.2 us -> 72.4 us (0.82); the launches traced: 86.8 us -> 72.1 us
  local copies, waits for them, and re-layouts: 7.33 us -> 0 us
  Pallas kernels: 77.6 us -> 71.5 us
  other arithmetic: 1.26 us -> 0 us
    unnamed x8 -> x0, local copies, waits for them, and re-layouts: 7.33 us -> none
    pallas_call x1 -> x2, Pallas kernels: 77.6 us -> 71.5 us  [the longest x1 62.1 us: on_device(): pl.pallas_call(main_kernel, out_shape=(jax.ShapeDtypeStruct((8, 8, 8, 128...]
    sub x1 -> x0, other arithmetic: 1.26 us -> none  [on_device(): local_col = (partner - (lon_n - 1 - lax.axis_index('lon')) * cols)[None, :]]
where the time goes in v3:
time: 72.4 us; the launch traced here: 72.1 us
  Pallas kernels  71.5 us (99%)
    pallas_call x1, Pallas kernels, on_device(): pl.pallas_call(main_kernel, out_shape=(jax.ShapeDtypeStruct((8, 8, 8, 128...  62.1 us
    pallas_call x1, Pallas kernels, on_device(): pl.pallas_call(functools.partial(last_kernel, scale), grid=(8,), out_shap...  9.35 us

profile of v3, /device:TPU:0, one launch (start us, length us, event | category | flops | bytes accessed | tf_op | source)
XLA Modules:
  0.0 72.1 jit_solution(10420060781497591874)
XLA Ops:
  0.6 62.1 %encoder_backward.1 = (f32[8,8,8,128]{3,2,1,0:T(8,128)}, bf16[4096,512]{1,0:T(8,128)(2,1)}) custom-call(bf16[672,512]{1,0:T(8,128)(2,1)} %bitcast.11, bf16[3072,512]{1,0:T(8,128)(2,1)} %bitcast.10, s32[32,512]{1,0:T(8,128)} %mask.3, s32[1,512]{1,0:T(1,128)} %bitcast.13, bf16[8192,256]{1,0:T(8,128)(2,1)} %bitcast.8, bf16[336,512]{1,0:T(8,128)(2,1)} %bitcast.12, ...), custom_call_target="tpu_custom_call" | custom-call | tf_op jit(solution)/shard_map/encoder_backward/pallas_call | solution.py:483
  62.8 9.3 %encoder_finish.1 = (f32[32,336]{1,0:T(8,128)}, f32[32,1536]{1,0:T(8,128)}, bf16[672,512]{1,0:T(8,128)(2,1)}, bf16[3072,512]{1,0:T(8,128)(2,1)}) custom-call(f32[8,8,8,128]{3,2,1,0:T(8,128)} %get-tuple-element.10.share, bf16[32,128,512]{2,1,0:T(8,128)(2,1)} %bitcast.9, s32[32,512]{1,0:T(8,128)} %mask.3), custom_call_target="tpu_custom_call" | custom-call | tf_op jit(solution)/shard_map/encoder_finish/pallas_call | solution.py:564

commit v4 on v3

--- a/solution.py
+++ b/solution.py
@@ -78,7 +78,7 @@
     loads.append(pltpu.make_async_copy(cot, craw, in_sem.at[7]))
     loads.append(pltpu.make_async_copy(wst, wspad.at[pl.ds(0, 336)], in_sem.at[8]))
     loads.append(pltpu.make_async_copy(wf, wstage, in_sem.at[9]))
-    for copy in loads:
+    for copy in loads[:7]:
         copy.start()
 
     barrier = pltpu.get_barrier_semaphore()
@@ -119,6 +119,9 @@
     for k in range(8):
         if k < 7:
             loads[k].wait()
+        if k == 3:
+            for copy in loads[7:]:
+                copy.start()
         x = raw[pl.ds(k * 512, 512), :].reshape(16, 32, 512) * mask_bf[None]
         y = dot(x.reshape(512, 512), perm[...]).astype(BF16)
         y = jnp.swapaxes(y.reshape(16, 32, 512), 0, 1)
@@ -240,27 +243,25 @@
         for copy in a_copies(p):
             copy.start()
 
-    def b_start():
-        for p in range(8):
-            k, slot = p % 3, p // 3
+    def b_start(k):
+        for p in range(k, 8, 3):
+            slot = p // 3
             for copy in a_copies(p):
                 copy.wait()
             own = rcore[(p,) + part(orders[k][0], spot[orders[k][0]])]
             got = recv_a[k][slot]
             sum_2[k][slot] = own + got[0] + got[1] + got[2]
-        for k in range(3):
-            for copy in b_copies(k):
-                copy.start()
-
-    def c_start():
-        for k in range(3):
-            for copy in b_copies(k):
-                copy.wait()
-            own = sum_2[k][(slice(None),) + part(orders[k][1], spot[orders[k][1]])]
-            got = recv_b[k][...]
-            sum_3[k][...] = own + got[0] + got[1] + got[2]
-            for copy in c_copies(k):
-                copy.start()
+        for copy in b_copies(k):
+            copy.start()
+
+    def c_start(k):
+        for copy in b_copies(k):
+            copy.wait()
+        own = sum_2[k][(slice(None),) + part(orders[k][1], spot[orders[k][1]])]
+        got = recv_b[k][...]
+        sum_3[k][...] = own + got[0] + got[1] + got[2]
+        for copy in c_copies(k):
+            copy.start()
 
     def g_start():
         for k in range(3):
@@ -274,15 +275,6 @@
         for copy in g_copies():
             copy.start()
 
-    def tile(n, pair):
-        _, parity, off = ROWS[n]
-        rows = planes[pl.ds((parity * 4 + pair * 2) * CP, 2 * CP), pl.ds(off * 256, 4096)]
-        return dot_nt(cot_a[...], rows)
-
-    core_start(0, tile(0, 0))
-    core_start(1, tile(1, 0))
-    a_start(0)
-
     fold_sel[...] = flag(down == partner[...] - (lon_n - 1 - lon) * 512)
 
     def folded(x, before, after):
@@ -311,6 +303,9 @@
     x_west = remote(6, sx, rxe, west)
     x_east.start()
     x_west.start()
+
+    core_start(0, tile(0, 0))
+    core_start(1, tile(1, 0))
 
     c_north.wait()
     c_south.wait()
@@ -331,9 +326,8 @@
     c_west.start()
 
     core_start(2, tile(2, 0))
-    a_start(1)
     core_start(3, tile(3, 0))
-    a_start(2)
+    a_start(0)
     x_east.wait()
     x_west.wait()
     side = jnp.concatenate(
@@ -347,7 +341,9 @@
         spread = jnp.where(first | last, 1.0, 0.0).astype(BF16)
         moved = dot(sc[...], spread).astype(BF16)
         core_start(4 + n, tile(n, 1) + dot_nt(moved, side))
-        a_start(3 + n)
+        a_start(1 + n)
+
+    a_start(5)
 
     loads[8].wait()
     loads[9].wait()
@@ -369,7 +365,7 @@
                     wcat[pl.ds((parity * 2 + q) * CP, CP), pl.ds((n * 2 + m) * 512, 512)] = wscr[
                         pl.ds((i * 4 + j) * CP, CP), :
                     ].astype(BF16)
-    a_start(7)
+    a_start(6)
 
     c_east.wait()
     c_west.wait()
@@ -393,6 +389,8 @@
             rows.append(jnp.concatenate([even, first, odd[:, 128:]], axis=1))
         return rows
 
+    a_start(7)
+
     fold, top = token_row(16, 2)
     sfold[...] = fold.astype(BF16)
     top_row[...] = top
@@ -411,10 +409,11 @@
         even, odd = token_row(s, 2)
         raw[pl.ds(pl.multiple_of(2 * s * CP, CP), CP), :] = even.astype(BF16)
         raw[pl.ds(pl.multiple_of((2 * s - 1) * CP, CP), CP), :] = odd.astype(BF16)
-        pl.when(s == 4)(b_start)
-        pl.when(s == 8)(c_start)
-        pl.when(s == 9)(lambda: out_copy(0, 0, 19).start())
-        pl.when(s == 12)(g_start)
+        for n, k in enumerate((2, 0, 1)):
+            pl.when(s == 3 + n)(functools.partial(b_start, k))
+            pl.when(s == 8 + n)(functools.partial(c_start, k))
+        pl.when(s == 10)(lambda: out_copy(0, 0, 19).start())
+        pl.when(s == 14)(g_start)
         return 0
 
     lax.fori_loop(1, 16, rows_of, 0)
@@ -437,40 +436,51 @@
     out_share.wait()
 
 
-def last_kernel(scale, share, rows, mask, ks_out, kf_out, xs_out, xf_out, permt2):
-    k = pl.program_id(0)
-
-    @pl.when(k == 0)
-    def _():
-        lane, across = iota((512, 1), 0), iota((1, 512), 1)
-        permt2[...] = flag(((2 * lane - lax.shift_right_logical(lane, 8)) & 511) == across)
-        turned = [None] * 16
-        for p in range(8):
-            for which in range(2):
-                o = ROWS[p % 4][0] * 4 + JORD[p // 4 * 2 + which]
-                own = [share[4 * which + y, p] for y in range(4)] + [jnp.zeros((96, 128), F32)]
-                turned[o] = jnp.transpose(jnp.concatenate(own, axis=0)) * scale
-        for n in range(15):
-            block = jnp.stack([x[n * 8:n * 8 + 8] for x in turned], axis=0)
-            block = jnp.transpose(jnp.swapaxes(block, 0, 1).reshape(128, 128))[:32]
-            if n < 12:
-                kf_out[:, pl.ds(n * 128, 128)] = block
-            elif n < 14:
-                ks_out[:, pl.ds((n - 12) * 128, 128)] = block
-            else:
-                ks_out[:, pl.ds(256, 80)] = block[:, :80]
-
-    x = jnp.swapaxes(rows[...], 0, 1).reshape(512, 512)
-    cells = dot(x, permt2[...]).astype(BF16).reshape(16, 32, 512)
-    cells = (cells * mask[...].astype(F32).astype(BF16)[None]).reshape(512, 512)
-
-    @pl.when(k < 6)
-    def _():
-        xf_out[...] = cells
-
-    @pl.when(k >= 6)
-    def _():
-        xs_out[...] = cells
+def last_kernel(scale, share, rows, mask, ks_out, kf_out, xs_out, xf_out, permt2, got, cells, own, ks, kf, in_sem, out_sem):
+    loads = [pltpu.make_async_copy(share, own, in_sem.at[8])]
+    for k in range(8):
+        block = pl.ds(k * 16, 16)
+        loads.append(pltpu.make_async_copy(rows.at[:, block], got.at[:, block], in_sem.at[k]))
+    for copy in loads:
+        copy.start()
+    lane, across = iota((512, 1), 0), iota((1, 512), 1)
+    permt2[...] = flag(((2 * lane - lax.shift_right_logical(lane, 8)) & 511) == across)
+    mask_bf = mask[...].astype(F32).astype(BF16)
+
+    loads[0].wait()
+    turned = [None] * 16
+    for p in range(8):
+        for which in range(2):
+            o = ROWS[p % 4][0] * 4 + JORD[p // 4 * 2 + which]
+            mine = [own[4 * which + y, p] for y in range(4)] + [jnp.zeros((96, 128), F32)]
+            turned[o] = jnp.transpose(jnp.concatenate(mine, axis=0)) * scale
+    for n in range(15):
+        block = jnp.stack([x[n * 8:n * 8 + 8] for x in turned], axis=0)
+        block = jnp.transpose(jnp.swapaxes(block, 0, 1).reshape(128, 128))[:32]
+        if n < 12:
+            kf[:, pl.ds(n * 128, 128)] = block
+        elif n < 14:
+            ks[:, pl.ds((n - 12) * 128, 128)] = block
+        else:
+            ks[:, pl.ds(256, 80)] = block[:, :80]
+    stores = [pltpu.make_async_copy(kf, kf_out, out_sem.at[8]), pltpu.make_async_copy(ks, ks_out, out_sem.at[9])]
+    for copy in stores:
+        copy.start()
+
+    for k in range(8):
+        loads[k + 1].wait()
+        x = jnp.swapaxes(got[:, pl.ds(k * 16, 16), :], 0, 1).reshape(512, 512)
+        y = dot(x, permt2[...]).astype(BF16).reshape(16, 32, 512) * mask_bf[None]
+        cells[pl.ds(k * 512, 512), :] = y.reshape(512, 512)
+        if k < 6:
+            dst, at, count = xf_out, k * 512, 512
+        else:
+            dst, at, count = xs_out, (k - 6) * 512, 512 if k == 6 else SC * 32 - 512
+        copy = pltpu.make_async_copy(cells.at[pl.ds(k * 512, count)], dst.at[pl.ds(at, count)], out_sem.at[k])
+        copy.start()
+        stores.append(copy)
+    for copy in stores:
+        copy.wait()
 
 
 def on_device(state, forcing, land_mask, partner, cotangent, weight_state, weight_force):
@@ -563,25 +573,25 @@
     own = width // (lat_n * batch_n)
     ks, kf, xs, xf = pl.pallas_call(
         functools.partial(last_kernel, scale),
-        grid=(8,),
         out_shape=(
             jax.ShapeDtypeStruct((own, sc * 16), F32),
             jax.ShapeDtypeStruct((own, fc * 16), F32),
             jax.ShapeDtypeStruct((sc * rows, cols), BF16),
             jax.ShapeDtypeStruct((fc * rows, cols), BF16),
         ),
-        in_specs=[
-            pl.BlockSpec((8, 8, 8, 128), lambda k: (0, 0, 0, 0)),
-            pl.BlockSpec((rows, 16, cols), lambda k: (0, k, 0)),
-            pl.BlockSpec((rows, cols), lambda k: (0, 0)),
+        in_specs=[any_spec, any_spec, vmem],
+        out_specs=(any_spec,) * 4,
+        scratch_shapes=[
+            pltpu.VMEM((512, 512), BF16),
+            pltpu.VMEM((rows, CP, cols), BF16),
+            pltpu.VMEM((rows * CP, cols), BF16),
+            pltpu.VMEM((8, 8, 8, 128), F32),
+            pltpu.VMEM((own, sc * 16), F32),
+            pltpu.VMEM((own, fc * 16), F32),
+            pltpu.SemaphoreType.DMA((9,)),
+            pltpu.SemaphoreType.DMA((10,)),
         ],
-        out_specs=(
-            pl.BlockSpec((own, sc * 16), lambda k: (0, 0)),
-            pl.BlockSpec((own, fc * 16), lambda k: (0, 0)),
-            pl.BlockSpec((16 * rows, cols), lambda k: (jnp.maximum(k - 6, 0), 0)),
-            pl.BlockSpec((16 * rows, cols), lambda k: (jnp.minimum(k, 5), 0)),
-        ),
-        scratch_shapes=[pltpu.VMEM((512, 512), BF16)],
+        compiler_params=pltpu.CompilerParams(vmem_limit_bytes=62 * 1024 * 1024),
         name="encoder_finish",
     )(share, cells.reshape(rows, CP, cols), land_mask)
     return (

time: 72.4 us -> 71.1 us (0.982)
  Pallas kernels: 71.5 us -> 70.1 us
    pallas_call x1, Pallas kernels: 9.35 us -> 6.93 us  [on_device(): pl.pallas_call(functools.partial(last_kernel, scale), out_shape=(jax.Shap...]
    pallas_call x1, Pallas kernels: 62.1 us -> 63.1 us  [on_device(): pl.pallas_call(main_kernel, out_shape=(jax.ShapeDtypeStruct((8, 8, 8, 128...]
where the time goes in v4:
time: 71.1 us; the launch traced here: 70.9 us
  Pallas kernels  70.1 us (99%)
  between operations  0.82 us (1%)
    pallas_call x1, Pallas kernels, on_device(): pl.pallas_call(main_kernel, out_shape=(jax.ShapeDtypeStruct((8, 8, 8, 128...  63.1 us
    pallas_call x1, Pallas kernels, on_device(): pl.pallas_call(functools.partial(last_kernel, scale), out_shape=(jax.Shap...  6.93 us

profile of v4, /device:TPU:0, one launch (start us, length us, event | category | flops | bytes accessed | tf_op | source)
XLA Modules:
  0.0 70.9 jit_solution(13794667937923144551)
XLA Ops:
  0.6 63.1 %encoder_backward.1 = (f32[8,8,8,128]{3,2,1,0:T(8,128)}, bf16[4096,512]{1,0:T(8,128)(2,1)}) custom-call(bf16[672,512]{1,0:T(8,128)(2,1)} %bitcast.11, bf16[3072,512]{1,0:T(8,128)(2,1)} %bitcast.10, s32[32,512]{1,0:T(8,128)} %mask.3, s32[1,512]{1,0:T(1,128)} %bitcast.13, bf16[8192,256]{1,0:T(8,128)(2,1)} %bitcast.8, bf16[336,512]{1,0:T(8,128)(2,1)} %bitcast.12, ...), custom_call_target="tpu_custom_call" | custom-call | tf_op jit(solution)/shard_map/encoder_backward/pallas_call | solution.py:493
  63.8 6.9 %encoder_finish.1 = (f32[32,336]{1,0:T(8,128)}, f32[32,1536]{1,0:T(8,128)}, bf16[672,512]{1,0:T(8,128)(2,1)}, bf16[3072,512]{1,0:T(8,128)(2,1)}) custom-call(f32[8,8,8,128]{3,2,1,0:T(8,128)} %get-tuple-element.10.share, bf16[32,128,512]{2,1,0:T(8,128)(2,1)} %bitcast.9, s32[32,512]{1,0:T(8,128)} %mask.3), custom_call_target="tpu_custom_call" | custom-call | tf_op jit(solution)/shard_map/encoder_finish/pallas_call | solution.py:574

commit v5 on v4

--- a/solution.py
+++ b/solution.py
@@ -233,9 +233,11 @@
             for d in range(1, 8)
         ]
 
-    def core_start(p, value):
-        gbuf[p] = value.reshape(4, 2, 2, 4, 8, 256)
-        core_copy(p).start()
+    def core_start(p, values):
+        for n, value in enumerate(values):
+            gbuf[p + n] = value.reshape(4, 2, 2, 4, 8, 256)
+        for n in range(len(values)):
+            core_copy(p + n).start()
 
     def a_start(p):
         core_copy(p).wait()
@@ -304,8 +306,7 @@
     x_east.start()
     x_west.start()
 
-    core_start(0, tile(0, 0))
-    core_start(1, tile(1, 0))
+    core_start(0, [tile(0, 0), tile(1, 0)])
 
     c_north.wait()
     c_south.wait()
@@ -325,24 +326,28 @@
     c_east.start()
     c_west.start()
 
-    core_start(2, tile(2, 0))
-    core_start(3, tile(3, 0))
+    core_start(2, [tile(2, 0), tile(3, 0)])
     a_start(0)
+    a_start(1)
     x_east.wait()
     x_west.wait()
     side = jnp.concatenate(
         [jnp.where(lane128 >= 64, rxw[...], zero16), jnp.where(lane128 < 64, rxe[...], zero16)], axis=0
     )
     lrow, lcol = iota((128, 128), 0), iota((128, 128), 1)
-    for n in range(4):
+
+    def side_tile(n):
         i = ROWS[n][0]
         first = (lrow >= 1) & (lrow <= 16) & (lcol == 62 + 2 * lrow + i)
         last = (lrow >= 65) & (lrow <= 80) & (lcol == 2 * lrow - 130 + i)
-        spread = jnp.where(first | last, 1.0, 0.0).astype(BF16)
-        moved = dot(sc[...], spread).astype(BF16)
-        core_start(4 + n, tile(n, 1) + dot_nt(moved, side))
-        a_start(1 + n)
-
+        moved = dot(sc[...], flag(first | last)).astype(BF16)
+        return tile(n, 1) + dot_nt(moved, side)
+
+    core_start(4, [side_tile(0), side_tile(1)])
+    a_start(2)
+    a_start(3)
+    core_start(6, [side_tile(2), side_tile(3)])
+    a_start(4)
     a_start(5)
 
     loads[8].wait()
@@ -366,6 +371,7 @@
                         pl.ds((i * 4 + j) * CP, CP), :
                     ].astype(BF16)
     a_start(6)
+    a_start(7)
 
     c_east.wait()
     c_west.wait()
@@ -388,8 +394,6 @@
             first = jnp.where(lane128 == 0, pltpu.roll(last[parity], lax.rem(128 - s, 128), 1), odd[:, :128])
             rows.append(jnp.concatenate([even, first, odd[:, 128:]], axis=1))
         return rows
-
-    a_start(7)
 
     fold, top = token_row(16, 2)
     sfold[...] = fold.astype(BF16)

time: 71.1 us -> 63.4 us (0.89)
  Pallas kernels: 70.1 us -> 62.4 us
    pallas_call x1, Pallas kernels: 63.1 us -> 55.5 us  [on_device(): pl.pallas_call(main_kernel, out_shape=(jax.ShapeDtypeStruct((8, 8, 8, 128...]
where the time goes in v5:
time: 63.4 us; the launch traced here: 63.2 us
  Pallas kernels  62.4 us (98%)
  between operations  0.82 us (1%)
    pallas_call x1, Pallas kernels, on_device(): pl.pallas_call(main_kernel, out_shape=(jax.ShapeDtypeStruct((8, 8, 8, 128...  55.5 us
    pallas_call x1, Pallas kernels, on_device(): pl.pallas_call(functools.partial(last_kernel, scale), out_shape=(jax.Shap...  6.93 us

profile of v5, /device:TPU:0, one launch (start us, length us, event | category | flops | bytes accessed | tf_op | source)
XLA Modules:
  0.0 63.2 jit_solution(17175729485361571564)
XLA Ops:
  0.6 55.5 %encoder_backward.1 = (f32[8,8,8,128]{3,2,1,0:T(8,128)}, bf16[4096,512]{1,0:T(8,128)(2,1)}) custom-call(bf16[672,512]{1,0:T(8,128)(2,1)} %bitcast.11, bf16[3072,512]{1,0:T(8,128)(2,1)} %bitcast.10, s32[32,512]{1,0:T(8,128)} %mask.3, s32[1,512]{1,0:T(1,128)} %bitcast.13, bf16[8192,256]{1,0:T(8,128)(2,1)} %bitcast.8, bf16[336,512]{1,0:T(8,128)(2,1)} %bitcast.12, ...), custom_call_target="tpu_custom_call" | custom-call | tf_op jit(solution)/shard_map/encoder_backward/pallas_call | solution.py:497
  56.1 6.9 %encoder_finish.1 = (f32[32,336]{1,0:T(8,128)}, f32[32,1536]{1,0:T(8,128)}, bf16[672,512]{1,0:T(8,128)(2,1)}, bf16[3072,512]{1,0:T(8,128)(2,1)}) custom-call(f32[8,8,8,128]{3,2,1,0:T(8,128)} %get-tuple-element.10.share, bf16[32,128,512]{2,1,0:T(8,128)(2,1)} %bitcast.9, s32[32,512]{1,0:T(8,128)} %mask.3), custom_call_target="tpu_custom_call" | custom-call | tf_op jit(solution)/shard_map/encoder_finish/pallas_call | solution.py:578

commit v6 on v5

--- a/solution.py
+++ b/solution.py
@@ -117,9 +117,10 @@
 
     lane16 = iota((16, 128), 1)
     for k in range(8):
-        if k < 7:
-            loads[k].wait()
-        if k == 3:
+        if k % 2 == 0:
+            for copy in loads[k:min(k + 2, 7)]:
+                copy.wait()
+        if k == 4:
             for copy in loads[7:]:
                 copy.start()
         x = raw[pl.ds(k * 512, 512), :].reshape(16, 32, 512) * mask_bf[None]
@@ -395,32 +396,42 @@
             rows.append(jnp.concatenate([even, first, odd[:, 128:]], axis=1))
         return rows
 
+    def keep(r, row):
+        raw[pl.ds(r * CP if isinstance(r, int) else pl.multiple_of(r * CP, CP), CP), :] = row.astype(BF16)
+
     fold, top = token_row(16, 2)
+    even, odd = token_row(15, 2)
+    (bottom,) = token_row(0, 1)
     sfold[...] = fold.astype(BF16)
     top_row[...] = top
+    keep(30, even)
+    keep(29, odd)
+    keep(0, bottom)
     g_mirror = remote(9, sfold, rfold, mirror)
 
     @pl.when(at_top)
     def _():
         g_mirror.start()
 
-    raw[pl.ds(0, CP), :] = token_row(0, 1)[0].astype(BF16)
-
     def out_copy(n, first, count):
         return pltpu.make_async_copy(raw.at[pl.ds(first * CP, count * CP)], rows_out.at[pl.ds(first * CP, count * CP)], out_sem.at[n])
 
-    def rows_of(s, _):
+    def rows_of(t, _):
+        s = 2 * t + 1
         even, odd = token_row(s, 2)
-        raw[pl.ds(pl.multiple_of(2 * s * CP, CP), CP), :] = even.astype(BF16)
-        raw[pl.ds(pl.multiple_of((2 * s - 1) * CP, CP), CP), :] = odd.astype(BF16)
-        for n, k in enumerate((2, 0, 1)):
-            pl.when(s == 3 + n)(functools.partial(b_start, k))
-            pl.when(s == 8 + n)(functools.partial(c_start, k))
-        pl.when(s == 10)(lambda: out_copy(0, 0, 19).start())
-        pl.when(s == 14)(g_start)
+        even_2, odd_2 = token_row(s + 1, 2)
+        keep(2 * s - 1, odd)
+        keep(2 * s, even)
+        keep(2 * s + 1, odd_2)
+        keep(2 * s + 2, even_2)
+        for k, b_at, c_at in ((2, 1, 3), (0, 1, 4), (1, 2, 4)):
+            pl.when(t == b_at)(functools.partial(b_start, k))
+            pl.when(t == c_at)(functools.partial(c_start, k))
+        pl.when(t == 5)(lambda: out_copy(0, 0, 19).start())
+        pl.when(t == 6)(g_start)
         return 0
 
-    lax.fori_loop(1, 16, rows_of, 0)
+    lax.fori_loop(0, 7, rows_of, 0)
     out_copy(1, 19, 12).start()
 
     @pl.when(at_top)
@@ -471,18 +482,22 @@
     for copy in stores:
         copy.start()
 
-    for k in range(8):
-        loads[k + 1].wait()
-        x = jnp.swapaxes(got[:, pl.ds(k * 16, 16), :], 0, 1).reshape(512, 512)
-        y = dot(x, permt2[...]).astype(BF16).reshape(16, 32, 512) * mask_bf[None]
-        cells[pl.ds(k * 512, 512), :] = y.reshape(512, 512)
-        if k < 6:
-            dst, at, count = xf_out, k * 512, 512
-        else:
-            dst, at, count = xs_out, (k - 6) * 512, 512 if k == 6 else SC * 32 - 512
-        copy = pltpu.make_async_copy(cells.at[pl.ds(k * 512, count)], dst.at[pl.ds(at, count)], out_sem.at[k])
-        copy.start()
-        stores.append(copy)
+    for pair in range(0, 8, 2):
+        copies = []
+        for copy in loads[pair + 1:pair + 3]:
+            copy.wait()
+        for k in (pair, pair + 1):
+            x = jnp.swapaxes(got[:, pl.ds(k * 16, 16), :], 0, 1).reshape(512, 512)
+            y = dot(x, permt2[...]).astype(BF16).reshape(16, 32, 512) * mask_bf[None]
+            cells[pl.ds(k * 512, 512), :] = y.reshape(512, 512)
+            if k < 6:
+                dst, at, count = xf_out, k * 512, 512
+            else:
+                dst, at, count = xs_out, (k - 6) * 512, 512 if k == 6 else SC * 32 - 512
+            copies.append(pltpu.make_async_copy(cells.at[pl.ds(k * 512, count)], dst.at[pl.ds(at, count)], out_sem.at[k]))
+        for copy in copies:
+            copy.start()
+        stores += copies
     for copy in stores:
         copy.wait()
 

time: 63.4 us -> 62.1 us (0.979)
  Pallas kernels: 62.4 us -> 61 us
    pallas_call x1, Pallas kernels: 55.5 us -> 54.6 us  [on_device(): pl.pallas_call(main_kernel, out_shape=(jax.ShapeDtypeStruct((8, 8, 8, 128...]
where the time goes in v6:
time: 62.1 us; the launch traced here: 61.9 us
  Pallas kernels  61 us (98%)
  between operations  0.82 us (1%)
    pallas_call x1, Pallas kernels, on_device(): pl.pallas_call(main_kernel, out_shape=(jax.ShapeDtypeStruct((8, 8, 8, 128...  54.6 us
    pallas_call x1, Pallas kernels, on_device(): pl.pallas_call(functools.partial(last_kernel, scale), out_shape=(jax.Shap...  6.41 us

profile of v6, /device:TPU:0, one launch (start us, length us, event | category | flops | bytes accessed | tf_op | source)
XLA Modules:
  0.0 61.9 jit_solution(15261733240816006024)
XLA Ops:
  0.6 54.6 %encoder_backward.1 = (f32[8,8,8,128]{3,2,1,0:T(8,128)}, bf16[4096,512]{1,0:T(8,128)(2,1)}) custom-call(bf16[672,512]{1,0:T(8,128)(2,1)} %bitcast.11, bf16[3072,512]{1,0:T(8,128)(2,1)} %bitcast.10, s32[32,512]{1,0:T(8,128)} %mask.3, s32[1,512]{1,0:T(1,128)} %bitcast.13, bf16[8192,256]{1,0:T(8,128)(2,1)} %bitcast.8, bf16[336,512]{1,0:T(8,128)(2,1)} %bitcast.12, ...), custom_call_target="tpu_custom_call" | custom-call | tf_op jit(solution)/shard_map/encoder_backward/pallas_call | solution.py:512
  55.3 6.4 %encoder_finish.1 = (f32[32,336]{1,0:T(8,128)}, f32[32,1536]{1,0:T(8,128)}, bf16[672,512]{1,0:T(8,128)(2,1)}, bf16[3072,512]{1,0:T(8,128)(2,1)}) custom-call(f32[8,8,8,128]{3,2,1,0:T(8,128)} %get-tuple-element.10.share, bf16[32,128,512]{2,1,0:T(8,128)(2,1)} %bitcast.9, s32[32,512]{1,0:T(8,128)} %mask.3), custom_call_target="tpu_custom_call" | custom-call | tf_op jit(solution)/shard_map/encoder_finish/pallas_call | solution.py:593

commit v7 on v6

--- a/solution.py
+++ b/solution.py
@@ -307,7 +307,6 @@
     x_east.start()
     x_west.start()
 
-    core_start(0, [tile(0, 0), tile(1, 0)])
 
     c_north.wait()
     c_south.wait()
@@ -327,7 +326,7 @@
     c_east.start()
     c_west.start()
 
-    core_start(2, [tile(2, 0), tile(3, 0)])
+    core_start(0, [tile(0, 0), tile(1, 0), tile(2, 0), tile(3, 0)])
     a_start(0)
     a_start(1)
     x_east.wait()
@@ -424,11 +423,11 @@
         keep(2 * s, even)
         keep(2 * s + 1, odd_2)
         keep(2 * s + 2, even_2)
-        for k, b_at, c_at in ((2, 1, 3), (0, 1, 4), (1, 2, 4)):
+        for k, b_at, c_at in ((2, 0, 2), (0, 0, 2), (1, 1, 3)):
             pl.when(t == b_at)(functools.partial(b_start, k))
             pl.when(t == c_at)(functools.partial(c_start, k))
-        pl.when(t == 5)(lambda: out_copy(0, 0, 19).start())
-        pl.when(t == 6)(g_start)
+        pl.when(t == 6)(lambda: out_copy(0, 0, 19).start())
+        pl.when(t == 5)(g_start)
         return 0
 
     lax.fori_loop(0, 7, rows_of, 0)

time: 62.1 us -> 65.7 us (1.058)
  Pallas kernels: 61 us -> 64.7 us
    pallas_call x1, Pallas kernels: 54.6 us -> 58.3 us  [on_device(): pl.pallas_call(main_kernel, out_shape=(jax.ShapeDtypeStruct((8, 8, 8, 128...]
where the time goes in v7:
time: 65.7 us; the launch traced here: 65.5 us
  Pallas kernels  64.7 us (98%)
  between operations  0.82 us (1%)
    pallas_call x1, Pallas kernels, on_device(): pl.pallas_call(main_kernel, out_shape=(jax.ShapeDtypeStruct((8, 8, 8, 128...  58.3 us
    pallas_call x1, Pallas kernels, on_device(): pl.pallas_call(functools.partial(last_kernel, scale), out_shape=(jax.Shap...  6.41 us

profile of v7, /device:TPU:0, one launch (start us, length us, event | category | flops | bytes accessed | tf_op | source)
XLA Modules:
  0.0 65.5 jit_solution(11249721065007919642)
XLA Ops:
  0.6 58.3 %encoder_backward.1 = (f32[8,8,8,128]{3,2,1,0:T(8,128)}, bf16[4096,512]{1,0:T(8,128)(2,1)}) custom-call(bf16[672,512]{1,0:T(8,128)(2,1)} %bitcast.11, bf16[3072,512]{1,0:T(8,128)(2,1)} %bitcast.10, s32[32,512]{1,0:T(8,128)} %mask.3, s32[1,512]{1,0:T(1,128)} %bitcast.13, bf16[8192,256]{1,0:T(8,128)(2,1)} %bitcast.8, bf16[336,512]{1,0:T(8,128)(2,1)} %bitcast.12, ...), custom_call_target="tpu_custom_call" | custom-call | tf_op jit(solution)/shard_map/encoder_backward/pallas_call | solution.py:511
  58.9 6.4 %encoder_finish.1 = (f32[32,336]{1,0:T(8,128)}, f32[32,1536]{1,0:T(8,128)}, bf16[672,512]{1,0:T(8,128)(2,1)}, bf16[3072,512]{1,0:T(8,128)(2,1)}) custom-call(f32[8,8,8,128]{3,2,1,0:T(8,128)} %get-tuple-element.10.share, bf16[32,128,512]{2,1,0:T(8,128)(2,1)} %bitcast.9, s32[32,512]{1,0:T(8,128)} %mask.3), custom_call_target="tpu_custom_call" | custom-call | tf_op jit(solution)/shard_map/encoder_finish/pallas_call | solution.py:592
